TPU v7x, 32 devices: a whole 2x2x4 slice. The times are simulated.
32 devices in a mesh: band: 4 (over x, core), grid: 8 (over z, y).
Axes of the slice: x: 2, y: 2, z: 4, core: 2. Of those that a mesh axis runs over, the one named last changes fastest.
Arguments:
- coefficients: bfloat16 [128, 16, 15360], P('grid', None, 'band'), may hold values from -6 to 6
- block_rows: int32 [128], P('grid'), may hold values from 5 to 16
- touch_atoms: int32 [16, 16], P('grid'), may hold values from 0 to 127, as said below
- basis_values: bfloat16 [16, 256, 640], P('grid'), may hold values from -0.375 to 0.375
- outer_field: float32 [16, 640], P('grid'), may hold values from -6 to 6
- occupations: float32 [15360], P('band'), may hold values from 0 to 2
Outputs:
- gradient: float32 [128, 16, 15360], P('grid', None, 'band')
- density: float32 [16, 640], P('grid')
Inputs may be any that keep to these rules, and one draw needn't show every extreme that they name: `touch_atoms`: each row names 16 different atoms. Among all entries of the 2 rows of one grid index, the atoms of each owner (atoms o * 16 to (o + 1) * 16 - 1) are named exactly 4 times or not at all.
All inputs are finite; a program needn't handle non-finite values.
Results may differ from a plain program's by a relative error of at most 0.0029.
Values may be sent and summed in bfloat16 or wider, within the bound.
No kernel may reach another device: no remote copies, remote signals or barrier semaphores. Data moves between devices by JAX's collectives and lax.ppermute only.
A program may use at most 128 MiB of HBM per device.

v0:
```python
import math

import jax
import jax.numpy as jnp
from jax import lax
from jax.sharding import PartitionSpec as P

exchange_coef = -0.9847450218426965


def band_width(count):
    return math.gcd(count, 768)


def forward_part(blocks, basis, weights, width):
    count = blocks.shape[1] // width

    def forward_step(index, carry):
        total, stored = carry
        part = lax.dynamic_slice_in_dim(blocks, index * width, width, 1)
        product = lax.dot_general(
            part, basis, (((0,), (0,)), ((), ())), preferred_element_type=jnp.float32
        )
        orbital = lax.optimization_barrier(product.astype(jnp.bfloat16))
        widened = orbital.astype(jnp.float32)
        scale = lax.dynamic_slice_in_dim(weights, index * width, width, 0)
        total = total + jnp.sum(scale[:, None] * widened * widened, axis=0)
        stored = lax.dynamic_update_slice_in_dim(stored, orbital, index * width, 0)
        return (total, stored)

    start = (
        jnp.zeros((basis.shape[1],), jnp.float32),
        jnp.zeros((blocks.shape[1], basis.shape[1]), jnp.bfloat16),
    )
    return lax.fori_loop(0, count, forward_step, start)


def backward_part(stored, basis, weights, potential, width):
    count = stored.shape[0] // width

    def backward_step(index, result):
        orbital = lax.dynamic_slice_in_dim(stored, index * width, width, 0).astype(jnp.float32)
        scale = lax.dynamic_slice_in_dim(weights, index * width, width, 0)
        wave = (scale[:, None] * potential[None, :] * orbital).astype(jnp.bfloat16)
        piece = lax.dot_general(
            basis, wave, (((1,), (1,)), ((), ())), preferred_element_type=jnp.float32
        )
        return lax.dynamic_update_slice_in_dim(result, piece.astype(jnp.bfloat16), index * width, 1)

    return lax.fori_loop(
        0, count, backward_step, jnp.zeros((basis.shape[0], stored.shape[0]), jnp.bfloat16)
    )


def body(coefficients, block_rows, touch_atoms, basis_values, outer_field, occupations):
    grid_size = lax.axis_size("grid")
    atom_dev, pad_rows, band_dev = coefficients.shape
    tiles_dev, touch_len = touch_atoms.shape
    entries = tiles_dev * touch_len
    capacity = max(2, (entries + grid_size - 1) // grid_size)
    all_bands = band_dev * lax.axis_size("band")
    width = band_width(band_dev)
    flat = touch_atoms.reshape(entries)
    owner = flat // atom_dev
    local = flat % atom_dev
    order = jnp.arange(entries, dtype=jnp.int32)
    tile_of = order // touch_len
    same = owner[:, None] == owner[None, :]
    earlier = order[None, :] < order[:, None]
    rank = jnp.sum(same & earlier, axis=1)
    same_tile = tile_of[:, None] == tile_of[None, :]
    tile_rank = jnp.sum(same & earlier & same_tile, axis=1)
    slot = owner * capacity + rank
    blank = jnp.full((grid_size * capacity,), -1, jnp.int32)
    ask_atom = blank.at[slot].set(local).reshape(grid_size, capacity)
    ask_tile = blank.at[slot].set(tile_of).reshape(grid_size, capacity)
    got_atom, got_tile = (
        lax.all_to_all(ask_atom, "grid", split_axis=0, concat_axis=0, tiled=True),
        lax.all_to_all(ask_tile, "grid", split_axis=0, concat_axis=0, tiled=True),
    )
    live = jnp.arange(pad_rows, dtype=jnp.int32)[None, :] < block_rows[:, None]
    masked = coefficients * live[:, :, None].astype(jnp.bfloat16)
    tile_blocks = []
    for tile in range(tiles_dev):
        before = jnp.sum((got_tile >= 0) & (got_tile < tile), axis=1)
        position = before[:, None] + jnp.arange(capacity, dtype=jnp.int32)[None, :]
        clipped = jnp.minimum(position, capacity - 1)
        src_atom = jnp.take_along_axis(got_atom, clipped, axis=1)
        src_tile = jnp.take_along_axis(got_tile, clipped, axis=1)
        valid = (position < capacity) & (src_tile == tile)
        rows = masked[jnp.maximum(src_atom, 0)]
        fetched = lax.all_to_all(
            rows * valid[:, :, None, None].astype(jnp.bfloat16),
            "grid",
            split_axis=0,
            concat_axis=0,
            tiled=True,
        )
        fetched = fetched.reshape(grid_size * capacity, pad_rows, band_dev)
        lower = tile * touch_len
        upper = (tile + 1) * touch_len
        chosen = owner[lower:upper] * capacity + tile_rank[lower:upper]
        tile_blocks.append(fetched[chosen].reshape(touch_len * pad_rows, band_dev))
    results = [
        forward_part(tile_blocks[t], basis_values[t], occupations, width) for t in range(tiles_dev)
    ]
    partial_value = jnp.stack([item[0] for item in results]) / all_bands
    orbitals = [item[1] for item in results]
    density = lax.psum(partial_value, "band")
    potential = outer_field + exchange_coef * jnp.cbrt(density)
    pieces = [
        backward_part(orbitals[t], basis_values[t], occupations, potential[t], width)
        for t in range(tiles_dev)
    ]
    projected = jnp.stack(pieces).reshape(entries, pad_rows, band_dev)
    outgoing = (
        jnp.zeros((grid_size * capacity, pad_rows, band_dev), jnp.bfloat16).at[slot].set(projected)
    )
    outgoing = outgoing.reshape(grid_size, capacity, pad_rows, band_dev)
    arrived = lax.all_to_all(outgoing, "grid", split_axis=0, concat_axis=0, tiled=True)
    selector = (
        got_atom.reshape(grid_size * capacity)[None, :]
        == jnp.arange(atom_dev, dtype=jnp.int32)[:, None]
    ).astype(jnp.bfloat16)
    total = jnp.dot(
        selector,
        arrived.reshape(grid_size * capacity, pad_rows * band_dev),
        preferred_element_type=jnp.float32,
    )
    gradient = total.reshape(atom_dev, pad_rows, band_dev) * live[:, :, None].astype(jnp.float32)
    return (gradient, density)


def solution(mesh):
    placed = (
        P("grid", None, "band"),
        P("grid"),
        P("grid", None),
        P("grid", None, None),
        P("grid", None),
        P("band"),
    )
    return jax.shard_map(
        body,
        mesh=mesh,
        in_specs=placed,
        out_specs=(P("grid", None, "band"), P("grid", None)),
        check_vma=False,
    )
```

profile of v0, /device:TPU:8, one launch (start us, length us, event | category | flops | bytes accessed | tf_op | source)
XLA Modules:
  0.0 380.7 jit_solution(5709949192476038634)
XLA Ops:
  3.7 6.3 %all-to-all-start.1 = ((s32[8,1,4]{2,1,0:T(1,128)}), s32[8,1,4]{2,1,0:T(1,128)S(1)}, u32[]{:S(2)}, u32[]{:S(2)}) async-start(s32[8,1,4]{2,1,0:T(1,128)} %bitcast.6), calls=%async_computation.1 | async-start | bytes 8192 | tf_op jit(solution)/shard_map/all_to_all | solution.py:79
  14.9 4.9 %all-to-all-start = ((s32[8,1,4]{2,1,0:T(1,128)}), s32[8,1,4]{2,1,0:T(1,128)S(1)}, u32[]{:S(2)}, u32[]{:S(2)}) async-start(s32[8,1,4]{2,1,0:T(1,128)} %bitcast.4), calls=%async_computation | async-start | bytes 8192 | tf_op jit(solution)/shard_map/all_to_all | solution.py:78
  20.1 4.6 %all-to-all-done = s32[8,1,4]{2,1,0:T(1,128)S(1)} async-done(((s32[8,1,4]{2,1,0:T(1,128)}), s32[8,1,4]{2,1,0:T(1,128)S(1)}, u32[]{:S(2)}, u32[]{:S(2)}) %all-to-all-start) | async-done | bytes 160 | tf_op jit(solution)/shard_map/all_to_all | solution.py:78
  27.0 2.7 gather_fusion
  29.7 4.4 %broadcast_multiply_fusion.1 = bf16[8,4,16,3840]{3,2,1,0:T(8,128)(2,1)} fusion(bf16[8,4,16,3840]{3,2,1,0:T(8,128)(2,1)} %bitcast.77, bf16[8,4]{1,0:T(8,128)(2,1)S(1)} %copy.74), kind=kLoop, calls=%fused_computation.46 | loop fusion | flops 1966080 | bytes 7864384 | tf_op jit(solution)/shard_map/mul | solution.py:93
  34.1 5.9 %all-to-all-start.2 = ((bf16[8,4,16,3840]{3,2,1,0:T(8,128)(2,1)}), bf16[8,4,16,3840]{3,2,1,0:T(8,128)(2,1)}, u32[]{:S(2)}, u32[]{:S(2)}) async-start(bf16[8,4,16,3840]{3,2,1,0:T(8,128)(2,1)} %broadcast_multiply_fusion.1), calls=%async_computation.2 | async-start | bytes 7864320 | tf_op jit(solution)/shard_map/all_to_all | solution.py:92
  42.0 2.7 gather_fusion.2
  45.0 4.4 %broadcast_multiply_fusion = bf16[8,4,16,3840]{3,2,1,0:T(8,128)(2,1)} fusion(bf16[8,4,16,3840]{3,2,1,0:T(8,128)(2,1)} %bitcast.76, bf16[8,4]{1,0:T(8,128)(2,1)S(1)} %copy.80), kind=kLoop, calls=%fused_computation.45 | loop fusion | flops 1966080 | bytes 7864384 | tf_op jit(solution)/shard_map/mul | solution.py:93
  49.3 74.0 %all-to-all-done.2 = bf16[8,4,16,3840]{3,2,1,0:T(8,128)(2,1)} async-done(((bf16[8,4,16,3840]{3,2,1,0:T(8,128)(2,1)}), bf16[8,4,16,3840]{3,2,1,0:T(8,128)(2,1)}, u32[]{:S(2)}, u32[]{:S(2)}) %all-to-all-start.2) | async-done | bytes 3932192 | tf_op jit(solution)/shard_map/all_to_all | solution.py:92
  123.4 7.0 %all-to-all-start.3 = ((bf16[8,4,16,3840]{3,2,1,0:T(8,128)(2,1)}), bf16[8,4,16,3840]{3,2,1,0:T(8,128)(2,1)}, u32[]{:S(2)}, u32[]{:S(2)}) async-start(bf16[8,4,16,3840]{3,2,1,0:T(8,128)(2,1)} %broadcast_multiply_fusion), calls=%async_computation.3 | async-start | bytes 7864320 | tf_op jit(solution)/shard_map/all_to_all | solution.py:92
  130.6 2.8 gather_fusion.1
  136.0 10.2 %while.60 = (s32[]{:T(128)}, f32[640]{0:T(1024)S(1)}, bf16[3840,640]{1,0:T(8,128)(2,1)}, f32[3840]{0:T(1024)S(1)}, bf16[256,3840]{1,0:T(8,128)(2,1)S(1)}, /*inde...) while((s32[]{:T(128)}, f32[640]{0:T(1024)S(1)}, ...), condition=%wide.region_7.9_spmd.clone, body=%wide.region_5.8_spmd.clone.sunk | while | flops 254116480 | bytes 4672681 | solution.py:35
  146.2 68.6 %all-to-all-done.3 = bf16[8,4,16,3840]{3,2,1,0:T(8,128)(2,1)} async-done(((bf16[8,4,16,3840]{3,2,1,0:T(8,128)(2,1)}), bf16[8,4,16,3840]{3,2,1,0:T(8,128)(2,1)}, u32[]{:S(2)}, u32[]{:S(2)}) %all-to-all-start.3) | async-done | bytes 3932192 | tf_op jit(solution)/shard_map/all_to_all | solution.py:92
  214.8 2.8 gather_fusion.3
  220.2 10.4 %while.61 = (s32[]{:T(128)}, f32[640]{0:T(1024)S(1)}, bf16[3840,640]{1,0:T(8,128)(2,1)}, f32[3840]{0:T(1024)S(1)}, bf16[256,3840]{1,0:T(8,128)(2,1)S(1)}, /*inde...) while((s32[]{:T(128)}, f32[640]{0:T(1024)S(1)}, ...), condition=%wide.region_11.13_spmd.clone, body=%wide.region_9.12_spmd.clone.sunk | while | flops 254116480 | bytes 4672681 | solution.py:35
  230.6 7.0 %psum.7 = f32[2,640]{1,0:T(2,128)S(1)} all-reduce(f32[2,640]{1,0:T(2,128)S(1)} %maximum_multiply_fusion), channel_id=1, replica_groups=mesh['band'=4,'grid'=8] {'band'}, use_global_device_ids=true, to_apply=%region_12.14 | all-reduce | flops 1280 | bytes 10240 | tf_op jit(solution)/shard_map/psum | solution.py:109
  238.2 10.3 %while.58 = (s32[]{:T(128)}, bf16[256,3840]{1,0:T(8,128)(2,1)S(1)}, f32[3840]{0:T(1024)S(1)}, f32[1,640]{1,0:T(1,128)S(1)}, bf16[3840,640]{1,0:T(8,128)(2,1)}, /...) while((s32[]{:T(128)}, bf16[256,3840]{1,0:T(8,128)(2,1)S(1)}, ...), condition=%wide.region_14.16_spmd, body=%wide.region_13.15_spmd.sunk | while | flops 253820928 | bytes 3293867 | solution.py:50
  250.0 13.9 %while.59 = (s32[]{:T(128)}, bf16[256,3840]{1,0:T(8,128)(2,1)}, f32[3840]{0:T(1024)S(1)}, f32[1,640]{1,0:T(1,128)S(1)}, bf16[3840,640]{1,0:T(8,128)(2,1)}, /*ind...) while((s32[]{:T(128)}, bf16[256,3840]{1,0:T(8,128)(2,1)}, ...), condition=%wide.region_16.18_spmd, body=%wide.region_15.17_spmd.sunk | while | flops 253820928 | bytes 3293867 | solution.py:50
  263.9 3.8 pad_maximum_fusion
  269.8 11.0 %scatter_fusion = bf16[32,16,3840]{2,1,0:T(8,128)(2,1)} fusion(bf16[32,16,3840]{2,1,0:T(8,128)(2,1)} %broadcast_in_dim.24, s32[32]{0:T(128)S(1)} %fusion.30, bf16[32,16,3840]{2,1,0:T(8,128)(2,1)} %bitcast.78), kind=kCustom, calls=%fused_computation.10 | custom fusion | bytes 11796608 | tf_op jit(solution)/shard_map/scatter | solution.py:117
  280.8 6.2 %all-to-all-start.4 = ((bf16[8,4,16,3840]{3,2,1,0:T(8,128)(2,1)}), bf16[8,4,16,3840]{3,2,1,0:T(8,128)(2,1)}, u32[]{:S(2)}, u32[]{:S(2)}) async-start(bf16[8,4,16,3840]{3,2,1,0:T(8,128)(2,1)} %bitcast.75), calls=%async_computation.4 | async-start | bytes 7864320 | tf_op jit(solution)/shard_map/all_to_all | solution.py:120
  288.3 83.7 %all-to-all-done.4 = bf16[8,4,16,3840]{3,2,1,0:T(8,128)(2,1)} async-done(((bf16[8,4,16,3840]{3,2,1,0:T(8,128)(2,1)}), bf16[8,4,16,3840]{3,2,1,0:T(8,128)(2,1)}, u32[]{:S(2)}, u32[]{:S(2)}) %all-to-all-start.4) | async-done | bytes 3932192 | tf_op jit(solution)/shard_map/all_to_all | solution.py:120
  372.0 4.5 %convolution_multiply_fusion = f32[16,16,3840]{2,0,1:T(8,128)S(1)} fusion(f32[16,16]{0,1:T(8,128)S(1)} %get-tuple-element.555, s32[32]{0:T(128)S(1)} %eq.52, bf16[4,8,16,3840]{3,2,1,0:T(8,128)(2,1)} %bitcast.31), kind=kOutput, calls=%fused_computation.41 | convolution fusion | flops 63898112 | bytes 7865472 | tf_op jit(solution)/shard_map/dot_general | solution.py:125
  376.5 4.2 %copy.84 = f32[16,16,3840]{2,1,0:T(8,128)} copy(f32[16,16,3840]{2,0,1:T(8,128)S(1)} %convolution_multiply_fusion) | data formatting | bytes 7864320
  (173 shorter events, 67.7 us)
Async XLA Ops:
  3.7 11.2 %all-to-all-start.1 = ((s32[8,1,4]{2,1,0:T(1,128)}), s32[8,1,4]{2,1,0:T(1,128)S(1)}, u32[]{:S(2)}, u32[]{:S(2)}) async-start(s32[8,1,4]{2,1,0:T(1,128)} %bitcast.6), calls=%async_computation.1 | async-start | bytes 8192 | tf_op jit(solution)/shard_map/all_to_all | solution.py:79
  14.9 9.9 %all-to-all-start = ((s32[8,1,4]{2,1,0:T(1,128)}), s32[8,1,4]{2,1,0:T(1,128)S(1)}, u32[]{:S(2)}, u32[]{:S(2)}) async-start(s32[8,1,4]{2,1,0:T(1,128)} %bitcast.4), calls=%async_computation | async-start | bytes 8192 | tf_op jit(solution)/shard_map/all_to_all | solution.py:78
  34.1 89.3 %all-to-all-start.2 = ((bf16[8,4,16,3840]{3,2,1,0:T(8,128)(2,1)}), bf16[8,4,16,3840]{3,2,1,0:T(8,128)(2,1)}, u32[]{:S(2)}, u32[]{:S(2)}) async-start(bf16[8,4,16,3840]{3,2,1,0:T(8,128)(2,1)} %broadcast_multiply_fusion.1), calls=%async_computation.2 | async-start | bytes 7864320 | tf_op jit(solution)/shard_map/all_to_all | solution.py:92
  49.3 81.2 %copy-start = (bf16[2,256,640]{2,1,0:T(8,128)(2,1)S(1)}, bf16[2,256,640]{2,1,0:T(8,128)(2,1)}, u32[]{:S(2)}) copy-start(bf16[2,256,640]{2,1,0:T(8,128)(2,1)} %param.19) | copy-start | bytes 1966084
  123.4 91.5 %all-to-all-start.3 = ((bf16[8,4,16,3840]{3,2,1,0:T(8,128)(2,1)}), bf16[8,4,16,3840]{3,2,1,0:T(8,128)(2,1)}, u32[]{:S(2)}, u32[]{:S(2)}) async-start(bf16[8,4,16,3840]{3,2,1,0:T(8,128)(2,1)} %broadcast_multiply_fusion), calls=%async_computation.3 | async-start | bytes 7864320 | tf_op jit(solution)/shard_map/all_to_all | solution.py:92
  130.6 5.4 %copy-start.1 = (f32[3840]{0:T(1024)S(1)}, f32[3840]{0:T(1024)}, u32[]{:S(2)}) copy-start(f32[3840]{0:T(1024)} %param.21) | copy-start | bytes 46084
  220.2 17.4 %copy-start.3 = (f32[2,640]{1,0:T(2,128)S(1)}, f32[2,640]{1,0:T(2,128)}, u32[]{:S(2)}) copy-start(f32[2,640]{1,0:T(2,128)} %param.20) | copy-start | bytes 15364
  237.6 0.6 copy-start.2
  280.8 91.2 %all-to-all-start.4 = ((bf16[8,4,16,3840]{3,2,1,0:T(8,128)(2,1)}), bf16[8,4,16,3840]{3,2,1,0:T(8,128)(2,1)}, u32[]{:S(2)}, u32[]{:S(2)}) async-start(bf16[8,4,16,3840]{3,2,1,0:T(8,128)(2,1)} %bitcast.75), calls=%async_computation.4 | async-start | bytes 7864320 | tf_op jit(solution)/shard_map/all_to_all | solution.py:120
where the time goes:
time: 386 us; the launch traced here: 381 us
  waiting for transfers between devices  232 us (60%)
  local copies, waits for them, and re-layouts  63.2 us (16%)
  starting transfers between devices  30.3 us (8%)
  matrix products  26.9 us (7%)
  other arithmetic  19.8 us (5%)
  blocking collectives  6.97 us (2%)
    all_to_all x2, waiting for transfers between devices, body(): lax.all_to_all(rows * valid[:, :, None, None].astype(jnp.bfloat16), 'grid...  143 us
    all_to_all x1, waiting for transfers between devices, body(): lax.all_to_all(outgoing, 'grid', split_axis=0, concat_axis=0, tiled=True)  83.7 us
    dot_general x10, matrix products, backward_step(): lax.dot_general(basis, wave, (((1,), (1,)), ((), ())), preferred_element_...  17.3 us
    all_to_all x2, starting transfers between devices, body(): lax.all_to_all(rows * valid[:, :, None, None].astype(jnp.bfloat16), 'grid...  12.9 us
    scatter x1, local copies, waits for them, and re-layouts, body(): jnp.zeros((grid_size * capacity, pad_rows, band_dev), jnp.bfloat16).at[slot]  11 us
    dynamic_update_slice x10, local copies, waits for them, and re-layouts, forward_step(): stored = lax.dynamic_update_slice_in_dim(stored, orbital, index * width, 0)  10.7 us
    mul x2, other arithmetic, body(): rows * valid[:, :, None, None].astype(jnp.bfloat16)  8.74 us
  transfers between devices with their start and end apart: 5, of which 5 were waited for; matrix products, arithmetic and copies ran while one was open for 8% of the time, Pallas kernels for 0%

commit v1 on v0

v1 whole, which is shorter than its diff:
```python
import functools

import jax
import jax.numpy as jnp
from jax import lax
from jax.experimental import pallas as pl
from jax.experimental.pallas import tpu as pltpu
from jax.sharding import PartitionSpec as P

exchange_coef = -0.9847450218426965
lanes = 128
big_vmem = 60 * 1024 * 1024


def pack_kernel(groups, per, rows_ref, me_ref, coef_ref, *out_refs):
    me = me_ref[0]
    atoms, pad, _ = coef_ref.shape
    row = lax.broadcasted_iota(jnp.int32, (pad, lanes), 0)
    for d, out_ref in enumerate(out_refs):
        peer = me ^ d
        for q in range(per):
            k = peer * per + q
            start = pl.multiple_of(jnp.minimum(k, groups - 1) * lanes, lanes)
            for a in range(atoms):
                value = coef_ref[a, :, pl.ds(start, lanes)]
                limit = jnp.where(k < groups, rows_ref[a], 0)
                out_ref[a * pad : (a + 1) * pad, q * lanes : (q + 1) * lanes] = jnp.where(
                    row < limit, value, jnp.zeros_like(value)
                )


def unpack_kernel(groups, per, rows_ref, me_ref, *refs):
    in_refs, out_ref = refs[:-1], refs[-1]
    me = me_ref[0]
    atoms, pad, _ = out_ref.shape
    row = lax.broadcasted_iota(jnp.int32, (pad, lanes), 0)
    for d, in_ref in enumerate(in_refs):
        peer = me ^ d
        for q in range(per):
            k = peer * per + q

            @pl.when(k < groups)
            def _():
                start = pl.multiple_of(k * lanes, lanes)
                for a in range(atoms):
                    value = in_ref[a * pad : (a + 1) * pad, q * lanes : (q + 1) * lanes]
                    out_ref[a, :, pl.ds(start, lanes)] = jnp.where(
                        row < rows_ref[a], value.astype(jnp.float32), 0.0
                    )


def load_all(me, beta, tile_count, block_refs, basis_refs, blocks, basis, sems):
    copies = []
    pieces = len(basis_refs)
    atoms = blocks.shape[0] // len(block_refs)
    for d, ref in enumerate(block_refs):
        owner = me ^ d
        copies.append(
            pltpu.make_async_copy(ref, blocks.at[pl.ds(owner * atoms, atoms)], sems.at[d])
        )
    for e, ref in enumerate(basis_refs):
        copies.append(
            pltpu.make_async_copy(ref, basis.at[:, beta ^ e], sems.at[len(block_refs) + e])
        )
    for copy in copies:
        copy.start()
    for copy in copies:
        copy.wait()


def tile_blocks(touch_ref, tile, blocks):
    touch_len = touch_ref.shape[1]
    return jnp.concatenate([blocks[touch_ref[tile, s]] for s in range(touch_len)], axis=0)


def tile_basis(tile, tiles_dev, basis):
    owners, pieces, piece, points = basis.shape
    per = pieces // tiles_dev
    part = basis[tile // tiles_dev, pl.ds((tile % tiles_dev) * per, per)]
    return part.reshape(per * piece, points)


def forward_kernel(n, m, tiles_dev, scale, touch_ref, at_ref, weight_ref, *refs):
    block_refs, basis_refs = refs[:n], refs[n : n + m]
    out_ref, blocks, basis, sems = refs[n + m :]
    me, beta = at_ref[0], at_ref[1]
    tile_count = touch_ref.shape[0]
    load_all(me, beta, tile_count, block_refs, basis_refs, blocks, basis, sems)

    def step(tile, carry):
        part = tile_blocks(touch_ref, tile, blocks)
        product = lax.dot_general(
            part,
            tile_basis(tile, tiles_dev, basis),
            (((0,), (0,)), ((), ())),
            preferred_element_type=jnp.float32,
        )
        orbital = product.astype(jnp.bfloat16).astype(jnp.float32)
        out_ref[pl.ds(tile, 1), :] = scale * jnp.sum(
            weight_ref[...] * orbital * orbital, axis=0, keepdims=True
        )
        return carry

    lax.fori_loop(0, tile_count, step, 0)


def backward_kernel(n, m, tiles_dev, touch_ref, at_ref, weight_ref, potential_ref, *refs):
    block_refs, basis_refs = refs[:n], refs[n : n + m]
    out_refs = refs[n + m : 2 * n + m]
    blocks, basis, total, sems = refs[2 * n + m :]
    me, beta = at_ref[0], at_ref[1]
    tile_count, touch_len = touch_ref.shape
    pad = blocks.shape[1]
    load_all(me, beta, tile_count, block_refs, basis_refs, blocks, basis, sems)
    total[...] = jnp.zeros_like(total)

    def step(tile, carry):
        part = tile_blocks(touch_ref, tile, blocks)
        values = tile_basis(tile, tiles_dev, basis)
        scaled = (values.astype(jnp.float32) * potential_ref[pl.ds(tile, 1), :]).astype(
            jnp.bfloat16
        )
        couple = lax.dot_general(
            scaled, values, (((1,), (1,)), ((), ())), preferred_element_type=jnp.float32
        )
        high = couple.astype(jnp.bfloat16)
        low = (couple - high.astype(jnp.float32)).astype(jnp.bfloat16)
        piece = jnp.dot(high, part, preferred_element_type=jnp.float32) + jnp.dot(
            low, part, preferred_element_type=jnp.float32
        )
        for s in range(touch_len):
            total[touch_ref[tile, s]] += piece[s * pad : (s + 1) * pad]
        return carry

    lax.fori_loop(0, tile_count, step, 0)
    weight = weight_ref[...]
    atoms = blocks.shape[0] // n
    for d, out_ref in enumerate(out_refs):
        owner = me ^ d
        for a in range(atoms):
            out_ref[a * pad : (a + 1) * pad, :] = (total[owner * atoms + a] * weight).astype(
                jnp.bfloat16
            )


smem = pl.BlockSpec(memory_space=pltpu.SMEM)
vmem = pl.BlockSpec(memory_space=pltpu.VMEM)
anywhere = pl.BlockSpec(memory_space=pl.ANY)


def swap(value, axis, offset):
    size = lax.axis_size(axis)
    return lax.ppermute(value, axis, [(i, i ^ offset) for i in range(size)])


def exchange(parts):
    return [parts[0]] + [swap(parts[d], "grid", d) for d in range(1, len(parts))]


def all_sum(value):
    for axis in ("band", "grid"):
        offset = 1
        while offset < lax.axis_size(axis):
            value = value + swap(value, axis, offset)
            offset *= 2
    return value


def body(coefficients, block_rows, touch_atoms, basis_values, outer_field, occupations):
    n = lax.axis_size("grid")
    m = lax.axis_size("band")
    me = lax.axis_index("grid").astype(jnp.int32)
    beta = lax.axis_index("band").astype(jnp.int32)
    atoms, pad, band_dev = coefficients.shape
    tiles_dev, touch_len = touch_atoms.shape
    points = basis_values.shape[2]
    slots = basis_values.shape[1]
    tile_count = tiles_dev * n
    groups = band_dev // lanes
    per = (groups + n - 1) // n
    width = per * lanes
    params = pltpu.CompilerParams(vmem_limit_bytes=big_vmem)
    at = jnp.stack([me, beta])

    touch_all = lax.all_gather(touch_atoms, "grid", axis=0, tiled=True)
    outer_all = lax.all_gather(outer_field, "grid", axis=0, tiled=True)

    piece = tiles_dev * slots // m
    own = lax.dynamic_slice_in_dim(
        basis_values.reshape(tiles_dev * slots, points), beta * piece, piece, 0
    )
    spread = lax.all_to_all(
        jnp.broadcast_to(own[None], (n, piece, points)), "grid", split_axis=0, concat_axis=0, tiled=True
    )

    sent = pl.pallas_call(
        functools.partial(pack_kernel, groups, per),
        out_shape=[jax.ShapeDtypeStruct((atoms * pad, width), jnp.bfloat16)] * n,
        in_specs=[smem, smem, vmem],
        out_specs=[vmem] * n,
        compiler_params=params,
        name="pack",
    )(block_rows, at, coefficients)
    got = [item.reshape(atoms, pad, width) for item in exchange(sent)]

    pieces = [spread]
    offset = m // 2
    order = [0]
    while offset:
        pieces = pieces + [swap(item, "band", offset) for item in pieces]
        order = order + [e ^ offset for e in order]
        offset //= 2
    basis = [pieces[order.index(e)] for e in range(m)]

    filled = jnp.pad(occupations, (0, n * width - band_dev))
    weight = lax.dynamic_slice_in_dim(filled, me * width, width, 0)
    all_bands = band_dev * m
    scratch = [
        pltpu.VMEM((n * atoms, pad, width), jnp.bfloat16),
        pltpu.VMEM((n, m, piece, points), jnp.bfloat16),
    ]
    sems = pltpu.SemaphoreType.DMA((n + m,))
    partial_value = pl.pallas_call(
        functools.partial(forward_kernel, n, m, tiles_dev, 1.0 / all_bands),
        out_shape=jax.ShapeDtypeStruct((tile_count, points), jnp.float32),
        in_specs=[smem, smem, vmem] + [anywhere] * (n + m),
        out_specs=vmem,
        scratch_shapes=scratch + [sems],
        compiler_params=params,
        name="forward",
    )(touch_all, at, weight[:, None], *got, *basis)
    density = all_sum(partial_value)
    potential = outer_all + exchange_coef * jnp.cbrt(density)
    back = pl.pallas_call(
        functools.partial(backward_kernel, n, m, tiles_dev),
        out_shape=[jax.ShapeDtypeStruct((atoms * pad, width), jnp.bfloat16)] * n,
        in_specs=[smem, smem, vmem, vmem] + [anywhere] * (n + m),
        out_specs=[vmem] * n,
        scratch_shapes=scratch + [pltpu.VMEM((n * atoms, pad, width), jnp.float32), sems],
        compiler_params=params,
        name="backward",
    )(touch_all, at, weight[None, :], potential, *got, *basis)
    returned = exchange(back)
    gradient = pl.pallas_call(
        functools.partial(unpack_kernel, groups, per),
        out_shape=jax.ShapeDtypeStruct((atoms, pad, band_dev), jnp.float32),
        in_specs=[smem, smem] + [vmem] * n,
        out_specs=vmem,
        compiler_params=params,
        name="unpack",
    )(block_rows, at, *returned)
    own_density = lax.dynamic_slice_in_dim(density, me * tiles_dev, tiles_dev, 0)
    return (gradient, own_density)


def solution(mesh):
    placed = (
        P("grid", None, "band"),
        P("grid"),
        P("grid", None),
        P("grid", None, None),
        P("grid", None),
        P("band"),
    )
    return jax.shard_map(
        body,
        mesh=mesh,
        in_specs=placed,
        out_specs=(P("grid", None, "band"), P("grid", None)),
        check_vma=False,
    )
```

time: 386 us -> 262 us (0.68); the launches traced: 381 us -> 261 us
  waiting for transfers between devices: 232 us -> 99.3 us
  blocking collectives: 6.97 us -> 94.7 us
  local copies, waits for them, and re-layouts: 63.2 us -> 4.18 us
  Pallas kernels: 0 us -> 36.8 us
  matrix products: 26.9 us -> 0 us
  other arithmetic: 19.8 us -> 2.21 us
  starting transfers between devices: 30.3 us -> 23.1 us
    all_to_all x5 -> x0, waiting for transfers between devices: 232 us -> none  [the longest x2 143 us: body(): lax.all_to_all(rows * valid[:, :, None, None].astype(jnp.bfloat16), 'grid...]
    ppermute x0 -> x22, waiting for transfers between devices: none -> 99.3 us  [swap(): return lax.ppermute(value, axis, [(i, i ^ offset) for i in range(size)])]
    all_gather x0 -> x2, blocking collectives: none -> 58.2 us  [the longest x1 29.3 us: body(): touch_all = lax.all_gather(touch_atoms, 'grid', axis=0, tiled=True)]
    pallas_call x0 -> x4, Pallas kernels: none -> 36.8 us  [the longest x1 17.7 us: body(): pl.pallas_call(functools.partial(backward_kernel, n, m, tiles_dev), out_s...]
    all_to_all x0 -> x1, blocking collectives: none -> 36.5 us  [body(): lax.all_to_all(jnp.broadcast_to(own[None], (n, piece, points)), 'grid', s...]
    all_to_all x5 -> x0, starting transfers between devices: 30.3 us -> none  [the longest x2 12.9 us: body(): lax.all_to_all(rows * valid[:, :, None, None].astype(jnp.bfloat16), 'grid...]
    dot_general x21 -> x0, matrix products: 26.9 us -> none  [the longest x10 17.3 us: backward_step(): lax.dot_general(basis, wave, (((1,), (1,)), ((), ())), preferred_element_...]
    ppermute x0 -> x22, starting transfers between devices: none -> 23.1 us  [swap(): return lax.ppermute(value, axis, [(i, i ^ offset) for i in range(size)])]
  transfers between devices with their start and end apart: 5 -> 22, of which waited for: 5 -> 15; matrix products, arithmetic and copies ran while one was open for 8% -> 1% of each run, Pallas kernels for 0% -> 1%
where the time goes in v1:
time: 262 us; the launch traced here: 261 us
  waiting for transfers between devices  99.3 us (38%)
  blocking collectives  94.7 us (36%)
  Pallas kernels  36.8 us (14%)
  starting transfers between devices  23.1 us (9%)
  local copies, waits for them, and re-layouts  4.18 us (2%)
    ppermute x22, waiting for transfers between devices, swap(): return lax.ppermute(value, axis, [(i, i ^ offset) for i in range(size)])  99.3 us
    all_to_all x1, blocking collectives, body(): lax.all_to_all(jnp.broadcast_to(own[None], (n, piece, points)), 'grid', s...  36.5 us
    all_gather x1, blocking collectives, body(): touch_all = lax.all_gather(touch_atoms, 'grid', axis=0, tiled=True)  29.3 us
    all_gather x1, blocking collectives, body(): outer_all = lax.all_gather(outer_field, 'grid', axis=0, tiled=True)  28.9 us
    ppermute x22, starting transfers between devices, swap(): return lax.ppermute(value, axis, [(i, i ^ offset) for i in range(size)])  23.1 us
    pallas_call x1, Pallas kernels, body(): pl.pallas_call(functools.partial(backward_kernel, n, m, tiles_dev), out_s...  17.7 us
    pallas_call x1, Pallas kernels, body(): pl.pallas_call(functools.partial(forward_kernel, n, m, tiles_dev, 1.0 / a...  11.8 us
  transfers between devices with their start and end apart: 22, of which 15 were waited for; matrix products, arithmetic and copies ran while one was open for 1% of the time, Pallas kernels for 1%

profile of v1, /device:TPU:8, one launch (start us, length us, event | category | flops | bytes accessed | tf_op | source)
XLA Modules:
  0.0 261.2 jit_solution(2826044782334779990)
XLA Ops:
  1.9 36.5 %all_to_all.5.refs_8_ = bf16[8,128,640]{2,1,0:T(8,128)(2,1)S(1)} all-to-all(bf16[8,128,640]{2,1,0:T(8,128)(2,1)S(1)} %broadcast_in_dim.14), channel_id=1, replica_groups=mesh['band'=4,'grid'=8] {'grid'}, dimensions={0} | all-to-all | bytes 2621440 | tf_op jit(solution)/shard_map/all_to_all | solution.py:192
  39.9 27.5 %collective-permute-done.8.refs_10_ = bf16[8,128,640]{2,1,0:T(8,128)(2,1)S(1)} collective-permute-done((bf16[8,128,640]{2,1,0:T(8,128)(2,1)S(1)}, bf16[8,128,640]{2,1,0:T(8,128)(2,1)S(1)}, u32[]{:S(2)}, u32[]{:S(2)}) %collective-permute-start.8) | collective-permute-done | bytes 1310752 | tf_op jit(solution)/shard_map/ppermute | solution.py:153
  68.2 3.4 %pack.1 = (bf16[256,512]{1,0:T(8,128)(2,1)}, bf16[256,512]{1,0:T(8,128)(2,1)}, bf16[256,512]{1,0:T(8,128)(2,1)}, bf16[256,512]{1,0:T(8,128)(2,1)}, bf16[256,512]...) custom-call(s32[16]{0:T(128)} %rows_ref.3, ...), custom_call_target="tpu_custom_call" | custom-call | tf_op jit(solution)/shard_map/pack/pallas_call | solution.py:196
  71.8 2.5 collective-permute-start.1
  75.0 5.4 %collective-permute-done = bf16[256,512]{1,0:T(8,128)(2,1)S(1)} collective-permute-done((bf16[256,512]{1,0:T(8,128)(2,1)}, bf16[256,512]{1,0:T(8,128)(2,1)S(1)}, u32[]{:S(2)}, u32[]{:S(2)}) %collective-permute-start) | collective-permute-done | bytes 262176 | tf_op jit(solution)/shard_map/ppermute | solution.py:153
  82.1 1.9 collective-permute-start.4
  84.0 5.9 %collective-permute-done.2 = bf16[256,512]{1,0:T(8,128)(2,1)} collective-permute-done((bf16[256,512]{1,0:T(8,128)(2,1)}, bf16[256,512]{1,0:T(8,128)(2,1)}, u32[]{:S(2)}, u32[]{:S(2)}) %collective-permute-start.2) | collective-permute-done | bytes 262176 | tf_op jit(solution)/shard_map/ppermute | solution.py:153
  90.8 15.2 %collective-permute-done.3 = bf16[256,512]{1,0:T(8,128)(2,1)} collective-permute-done((bf16[256,512]{1,0:T(8,128)(2,1)}, bf16[256,512]{1,0:T(8,128)(2,1)}, u32[]{:S(2)}, u32[]{:S(2)}) %collective-permute-start.3) | collective-permute-done | bytes 262176 | tf_op jit(solution)/shard_map/ppermute | solution.py:153
  106.0 1.9 collective-permute-start.6
  109.6 29.3 %all-gather = s32[8,2,16]{2,1,0:T(2,128)} all-gather(s32[1,2,16]{2,1,0:T(2,128)S(1)} %bitcast.26), channel_id=1, replica_groups=mesh['band'=4,'grid'=8] {'grid'}, dimensions={0}, use_global_device_ids=true | all-gather | bytes 1152 | tf_op jit(solution)/shard_map/all_gather | solution.py:185
  138.9 11.8 %forward.1 = f32[16,640]{1,0:T(8,128)} custom-call(s32[16,16]{1,0:T(8,128)} %bitcast.21, s32[2]{0:T(128)} %pad_add_fusion.me_ref.at_ref, f32[512,1]{1,0:T(8,128)} %copy.9.weight_ref, bf16[16,16,512]{2,1,0:T(8,128)(2,1)} %bitcast.17, bf16[16,16,512]{2,1,0:T(8,128)(2,1)} %bitcast.19, bf16[16,16,512]{2,1,0:T(8,128)(2,1)} %bitcast.9.refs_2_, ...), custom_call_target="tpu_custom_call" | custom-call | tf_op jit(solution)/shard_map/forward/pallas_call | solution.py:223
  154.5 2.5 collective-permute-done.11
  157.7 3.3 %collective-permute-done.12 = f32[16,640]{1,0:T(8,128)S(1)} collective-permute-done((f32[16,640]{1,0:T(8,128)S(1)}, f32[16,640]{1,0:T(8,128)S(1)}, u32[]{:S(2)}, u32[]{:S(2)}) %collective-permute-start.12) | collective-permute-done | bytes 40992 | tf_op jit(solution)/shard_map/ppermute | solution.py:153
  161.0 4.2 %collective-permute-done.13 = f32[16,640]{1,0:T(8,128)S(1)} collective-permute-done((f32[16,640]{1,0:T(8,128)S(1)}, f32[16,640]{1,0:T(8,128)S(1)}, u32[]{:S(2)}, u32[]{:S(2)}) %collective-permute-start.13) | collective-permute-done | bytes 40992 | tf_op jit(solution)/shard_map/ppermute | solution.py:153
  166.5 28.9 %all-gather.1 = f32[8,2,640]{2,1,0:T(2,128)S(1)} all-gather(f32[1,2,640]{2,1,0:T(2,128)S(1)} %bitcast.25), channel_id=1, replica_groups=mesh['band'=4,'grid'=8] {'grid'}, dimensions={0}, use_global_device_ids=true | all-gather | bytes 46080 | tf_op jit(solution)/shard_map/all_gather | solution.py:186
  196.1 17.7 %backward.1 = (bf16[256,512]{1,0:T(8,128)(2,1)}, bf16[256,512]{1,0:T(8,128)(2,1)}, bf16[256,512]{1,0:T(8,128)(2,1)}, bf16[256,512]{1,0:T(8,128)(2,1)}, bf16[256,...) custom-call(s32[16,16]{1,0:T(8,128)} %bitcast.22, ...), custom_call_target="tpu_custom_call" | custom-call | tf_op jit(solution)/shard_map/backward/pallas_call | solution.py:234
  213.9 3.2 %collective-permute-start.16 = (bf16[256,512]{1,0:T(8,128)(2,1)}, bf16[256,512]{1,0:T(8,128)(2,1)S(1)}, u32[]{:S(2)}, u32[]{:S(2)}) collective-permute-start(bf16[256,512]{1,0:T(8,128)(2,1)} %get-tuple-element.28), channel_id=1, source_target_pairs={{0,2},{1,3},{2,0},{3,1},{4,6},{5,7},{6,4},{7,5},{8,10},{9,11},{10,... | collective-permute-start | bytes 786440 | tf_op jit(solution)/shard_map/ppermute | solution.py:153
  222.8 8.9 %collective-permute-done.16.refs_2_ = bf16[256,512]{1,0:T(8,128)(2,1)S(1)} collective-permute-done((bf16[256,512]{1,0:T(8,128)(2,1)}, bf16[256,512]{1,0:T(8,128)(2,1)S(1)}, u32[]{:S(2)}, u32[]{:S(2)}) %collective-permute-start.16) | collective-permute-done | bytes 262176 | tf_op jit(solution)/shard_map/ppermute | solution.py:153
  232.4 2.2 collective-permute-done.17.refs_3_
  234.5 7.8 %collective-permute-done.18.refs_4_ = bf16[256,512]{1,0:T(8,128)(2,1)S(1)} collective-permute-done((bf16[256,512]{1,0:T(8,128)(2,1)}, bf16[256,512]{1,0:T(8,128)(2,1)S(1)}, u32[]{:S(2)}, u32[]{:S(2)}) %collective-permute-start.18) | collective-permute-done | bytes 262176 | tf_op jit(solution)/shard_map/ppermute | solution.py:153
  242.3 5.6 %collective-permute-done.19.refs_5_ = bf16[256,512]{1,0:T(8,128)(2,1)S(1)} collective-permute-done((bf16[256,512]{1,0:T(8,128)(2,1)}, bf16[256,512]{1,0:T(8,128)(2,1)S(1)}, u32[]{:S(2)}, u32[]{:S(2)}) %collective-permute-start.19) | collective-permute-done | bytes 262176 | tf_op jit(solution)/shard_map/ppermute | solution.py:153
  247.9 5.9 %collective-permute-done.20.refs_6_ = bf16[256,512]{1,0:T(8,128)(2,1)S(1)} collective-permute-done((bf16[256,512]{1,0:T(8,128)(2,1)}, bf16[256,512]{1,0:T(8,128)(2,1)S(1)}, u32[]{:S(2)}, u32[]{:S(2)}) %collective-permute-start.20) | collective-permute-done | bytes 262176 | tf_op jit(solution)/shard_map/ppermute | solution.py:153
  253.8 2.6 collective-permute-done.21.refs_7_
  257.1 4.0 %unpack.1 = f32[16,16,3840]{2,1,0:T(8,128)} custom-call(s32[16]{0:T(128)} %rows_ref.3, s32[2]{0:T(128)} %pad_add_fusion.me_ref.at_ref, bf16[256,512]{1,0:T(8,128)(2,1)} %get-tuple-element.26.refs_0_, bf16[256,512]{1,0:T(8,128)(2,1)} %copy-done.4, bf16[256,512]{1,0:T(8,128)(2,1)} %copy-done.5, bf16[256,512]{1,0:T(8,128)(2,1)} %copy-done.6, ...), custom_call_target="tpu_custom_call" | custom-call | tf_op jit(solution)/shard_map/unpack/pallas_call | solution.py:244
  (67 shorter events, 22.3 us)
Async XLA Ops:
  38.4 100.4 %copy-start.1 = (bf16[8,128,640]{2,1,0:T(8,128)(2,1)}, bf16[8,128,640]{2,1,0:T(8,128)(2,1)S(1)}, u32[]{:S(2)}) copy-start(bf16[8,128,640]{2,1,0:T(8,128)(2,1)S(1)} %all_to_all.5.refs_8_) | copy-start | bytes 3932164
  38.4 29.0 %collective-permute-start.8 = (bf16[8,128,640]{2,1,0:T(8,128)(2,1)S(1)}, bf16[8,128,640]{2,1,0:T(8,128)(2,1)S(1)}, u32[]{:S(2)}, u32[]{:S(2)}) collective-permute-start(bf16[8,128,640]{2,1,0:T(8,128)(2,1)S(1)} %all_to_all.5.refs_8_), channel_id=1, source_target_pairs={{0,16},{8,24},{16,0},{24,8},{1,17},{9,25},{17,1},{25,9},{2,18},{10... | collective-permute-start | bytes 3932168 | tf_op jit(solution)/shard_map/ppermute | solution.py:153
  39.9 98.9 %collective-permute-start.7 = (bf16[8,128,640]{2,1,0:T(8,128)(2,1)S(1)}, bf16[8,128,640]{2,1,0:T(8,128)(2,1)}, u32[]{:S(2)}, u32[]{:S(2)}) collective-permute-start(bf16[8,128,640]{2,1,0:T(8,128)(2,1)S(1)} %all_to_all.5.refs_8_), channel_id=1, source_target_pairs={{0,8},{8,0},{16,24},{24,16},{1,9},{9,1},{17,25},{25,17},{2,10},{10... | collective-permute-start | bytes 3932168 | tf_op jit(solution)/shard_map/ppermute | solution.py:153
  67.4 71.4 %copy-start.2 = (bf16[8,128,640]{2,1,0:T(8,128)(2,1)}, bf16[8,128,640]{2,1,0:T(8,128)(2,1)S(1)}, u32[]{:S(2)}) copy-start(bf16[8,128,640]{2,1,0:T(8,128)(2,1)S(1)} %collective-permute-done.8.refs_10_) | copy-start | bytes 3932164
  67.4 71.4 %collective-permute-start.9 = (bf16[8,128,640]{2,1,0:T(8,128)(2,1)S(1)}, bf16[8,128,640]{2,1,0:T(8,128)(2,1)}, u32[]{:S(2)}, u32[]{:S(2)}) collective-permute-start(bf16[8,128,640]{2,1,0:T(8,128)(2,1)S(1)} %collective-permute-done.8.refs_10_), channel_id=1, source_target_pairs={{0,8},{8,0},{16,24},{24,16},{1,9},{9,1},{17,25},{25,17},{2,10},{10... | collective-permute-start | bytes 3932168 | tf_op jit(solution)/shard_map/ppermute | solution.py:153
  71.5 8.9 %collective-permute-start = (bf16[256,512]{1,0:T(8,128)(2,1)}, bf16[256,512]{1,0:T(8,128)(2,1)S(1)}, u32[]{:S(2)}, u32[]{:S(2)}) collective-permute-start(bf16[256,512]{1,0:T(8,128)(2,1)} %get-tuple-element.19), channel_id=1, source_target_pairs={{0,1},{1,0},{2,3},{3,2},{4,5},{5,4},{6,7},{7,6},{8,9},{9,8},{10,11... | collective-permute-start | bytes 786440 | tf_op jit(solution)/shard_map/ppermute | solution.py:153
  71.8 10.3 %collective-permute-start.1 = (bf16[256,512]{1,0:T(8,128)(2,1)}, bf16[256,512]{1,0:T(8,128)(2,1)}, u32[]{:S(2)}, u32[]{:S(2)}) collective-permute-start(bf16[256,512]{1,0:T(8,128)(2,1)} %get-tuple-element.20), channel_id=1, source_target_pairs={{0,2},{1,3},{2,0},{3,1},{4,6},{5,7},{6,4},{7,5},{8,10},{9,11},{10,... | collective-permute-start | bytes 786440 | tf_op jit(solution)/shard_map/ppermute | solution.py:153
  74.3 15.7 %collective-permute-start.2 = (bf16[256,512]{1,0:T(8,128)(2,1)}, bf16[256,512]{1,0:T(8,128)(2,1)}, u32[]{:S(2)}, u32[]{:S(2)}) collective-permute-start(bf16[256,512]{1,0:T(8,128)(2,1)} %get-tuple-element.21), channel_id=1, source_target_pairs={{0,3},{1,2},{2,1},{3,0},{4,7},{5,6},{6,5},{7,4},{8,11},{9,10},{10,... | collective-permute-start | bytes 786440 | tf_op jit(solution)/shard_map/ppermute | solution.py:153
  80.4 25.6 %collective-permute-start.3 = (bf16[256,512]{1,0:T(8,128)(2,1)}, bf16[256,512]{1,0:T(8,128)(2,1)}, u32[]{:S(2)}, u32[]{:S(2)}) collective-permute-start(bf16[256,512]{1,0:T(8,128)(2,1)} %get-tuple-element.22), channel_id=1, source_target_pairs={{0,4},{1,5},{2,6},{3,7},{4,0},{5,1},{6,2},{7,3},{8,12},{9,13},{10,... | collective-permute-start | bytes 786440 | tf_op jit(solution)/shard_map/ppermute | solution.py:153
  82.1 56.7 %collective-permute-start.4 = (bf16[256,512]{1,0:T(8,128)(2,1)}, bf16[256,512]{1,0:T(8,128)(2,1)}, u32[]{:S(2)}, u32[]{:S(2)}) collective-permute-start(bf16[256,512]{1,0:T(8,128)(2,1)} %get-tuple-element.23), channel_id=1, source_target_pairs={{0,5},{1,4},{2,7},{3,6},{4,1},{5,0},{6,3},{7,2},{8,13},{9,12},{10,... | collective-permute-start | bytes 786440 | tf_op jit(solution)/shard_map/ppermute | solution.py:153
  89.9 48.9 %collective-permute-start.5 = (bf16[256,512]{1,0:T(8,128)(2,1)}, bf16[256,512]{1,0:T(8,128)(2,1)}, u32[]{:S(2)}, u32[]{:S(2)}) collective-permute-start(bf16[256,512]{1,0:T(8,128)(2,1)} %get-tuple-element.24), channel_id=1, source_target_pairs={{0,6},{1,7},{2,4},{3,5},{4,2},{5,3},{6,0},{7,1},{8,14},{9,15},{10,... | collective-permute-start | bytes 786440 | tf_op jit(solution)/shard_map/ppermute | solution.py:153
  106.0 32.8 %collective-permute-start.6 = (bf16[256,512]{1,0:T(8,128)(2,1)}, bf16[256,512]{1,0:T(8,128)(2,1)}, u32[]{:S(2)}, u32[]{:S(2)}) collective-permute-start(bf16[256,512]{1,0:T(8,128)(2,1)} %get-tuple-element.25), channel_id=1, source_target_pairs={{0,7},{1,6},{2,5},{3,4},{4,3},{5,2},{6,1},{7,0},{8,15},{9,14},{10,... | collective-permute-start | bytes 786440 | tf_op jit(solution)/shard_map/ppermute | solution.py:153
  150.7 1.5 collective-permute-start.10
  153.0 4.0 %collective-permute-start.11 = (f32[16,640]{1,0:T(8,128)S(1)}, f32[16,640]{1,0:T(8,128)S(1)}, u32[]{:S(2)}, u32[]{:S(2)}) collective-permute-start(f32[16,640]{1,0:T(8,128)S(1)} %add.31), channel_id=1, source_target_pairs={{0,16},{8,24},{16,0},{24,8},{1,17},{9,25},{17,1},{25,9},{2,18},{10... | collective-permute-start | bytes 122888 | tf_op jit(solution)/shard_map/ppermute | solution.py:153
  157.0 4.0 %collective-permute-start.12 = (f32[16,640]{1,0:T(8,128)S(1)}, f32[16,640]{1,0:T(8,128)S(1)}, u32[]{:S(2)}, u32[]{:S(2)}) collective-permute-start(f32[16,640]{1,0:T(8,128)S(1)} %add.32), channel_id=1, source_target_pairs={{0,1},{1,0},{2,3},{3,2},{4,5},{5,4},{6,7},{7,6},{8,9},{9,8},{10,11... | collective-permute-start | bytes 122888 | tf_op jit(solution)/shard_map/ppermute | solution.py:153
  161.0 4.2 %collective-permute-start.13 = (f32[16,640]{1,0:T(8,128)S(1)}, f32[16,640]{1,0:T(8,128)S(1)}, u32[]{:S(2)}, u32[]{:S(2)}) collective-permute-start(f32[16,640]{1,0:T(8,128)S(1)} %add.33), channel_id=1, source_target_pairs={{0,2},{1,3},{2,0},{3,1},{4,6},{5,7},{6,4},{7,5},{8,10},{9,11},{10,... | collective-permute-start | bytes 122888 | tf_op jit(solution)/shard_map/ppermute | solution.py:153
  165.2 30.3 %collective-permute-start.14 = (f32[16,640]{1,0:T(8,128)S(1)}, f32[16,640]{1,0:T(8,128)S(1)}, u32[]{:S(2)}, u32[]{:S(2)}) collective-permute-start(f32[16,640]{1,0:T(8,128)S(1)} %add.34), channel_id=1, source_target_pairs={{0,4},{1,5},{2,6},{3,7},{4,0},{5,1},{6,2},{7,3},{8,12},{9,13},{10,... | collective-permute-start | bytes 122888 | tf_op jit(solution)/shard_map/ppermute | solution.py:153
  213.8 8.6 %collective-permute-start.15 = (bf16[256,512]{1,0:T(8,128)(2,1)}, bf16[256,512]{1,0:T(8,128)(2,1)S(1)}, u32[]{:S(2)}, u32[]{:S(2)}) collective-permute-start(bf16[256,512]{1,0:T(8,128)(2,1)} %get-tuple-element.27), channel_id=1, source_target_pairs={{0,1},{1,0},{2,3},{3,2},{4,5},{5,4},{6,7},{7,6},{8,9},{9,8},{10,11... | collective-permute-start | bytes 786440 | tf_op jit(solution)/shard_map/ppermute | solution.py:153
  213.9 17.9 %collective-permute-start.16 = (bf16[256,512]{1,0:T(8,128)(2,1)}, bf16[256,512]{1,0:T(8,128)(2,1)S(1)}, u32[]{:S(2)}, u32[]{:S(2)}) collective-permute-start(bf16[256,512]{1,0:T(8,128)(2,1)} %get-tuple-element.28), channel_id=1, source_target_pairs={{0,2},{1,3},{2,0},{3,1},{4,6},{5,7},{6,4},{7,5},{8,10},{9,11},{10,... | collective-permute-start | bytes 786440 | tf_op jit(solution)/shard_map/ppermute | solution.py:153
  217.1 17.4 %collective-permute-start.17 = (bf16[256,512]{1,0:T(8,128)(2,1)}, bf16[256,512]{1,0:T(8,128)(2,1)S(1)}, u32[]{:S(2)}, u32[]{:S(2)}) collective-permute-start(bf16[256,512]{1,0:T(8,128)(2,1)} %get-tuple-element.29), channel_id=1, source_target_pairs={{0,3},{1,2},{2,1},{3,0},{4,7},{5,6},{6,5},{7,4},{8,11},{9,10},{10,... | collective-permute-start | bytes 786440 | tf_op jit(solution)/shard_map/ppermute | solution.py:153
  218.5 23.8 %collective-permute-start.18 = (bf16[256,512]{1,0:T(8,128)(2,1)}, bf16[256,512]{1,0:T(8,128)(2,1)S(1)}, u32[]{:S(2)}, u32[]{:S(2)}) collective-permute-start(bf16[256,512]{1,0:T(8,128)(2,1)} %get-tuple-element.30), channel_id=1, source_target_pairs={{0,4},{1,5},{2,6},{3,7},{4,0},{5,1},{6,2},{7,3},{8,12},{9,13},{10,... | collective-permute-start | bytes 786440 | tf_op jit(solution)/shard_map/ppermute | solution.py:153
  219.6 28.3 %collective-permute-start.19 = (bf16[256,512]{1,0:T(8,128)(2,1)}, bf16[256,512]{1,0:T(8,128)(2,1)S(1)}, u32[]{:S(2)}, u32[]{:S(2)}) collective-permute-start(bf16[256,512]{1,0:T(8,128)(2,1)} %get-tuple-element.31), channel_id=1, source_target_pairs={{0,5},{1,4},{2,7},{3,6},{4,1},{5,0},{6,3},{7,2},{8,13},{9,12},{10,... | collective-permute-start | bytes 786440 | tf_op jit(solution)/shard_map/ppermute | solution.py:153
  222.3 31.5 %collective-permute-start.20 = (bf16[256,512]{1,0:T(8,128)(2,1)}, bf16[256,512]{1,0:T(8,128)(2,1)S(1)}, u32[]{:S(2)}, u32[]{:S(2)}) collective-permute-start(bf16[256,512]{1,0:T(8,128)(2,1)} %get-tuple-element.32), channel_id=1, source_target_pairs={{0,6},{1,7},{2,4},{3,5},{4,2},{5,3},{6,0},{7,1},{8,14},{9,15},{10,... | collective-permute-start | bytes 786440 | tf_op jit(solution)/shard_map/ppermute | solution.py:153
  231.7 24.7 %collective-permute-start.21 = (bf16[256,512]{1,0:T(8,128)(2,1)}, bf16[256,512]{1,0:T(8,128)(2,1)S(1)}, u32[]{:S(2)}, u32[]{:S(2)}) collective-permute-start(bf16[256,512]{1,0:T(8,128)(2,1)} %get-tuple-element.33), channel_id=1, source_target_pairs={{0,7},{1,6},{2,5},{3,4},{4,3},{5,2},{6,1},{7,0},{8,15},{9,14},{10,... | collective-permute-start | bytes 786440 | tf_op jit(solution)/shard_map/ppermute | solution.py:153
  (12 other events, 307.0 us)

commit v2 on v1

v2 whole, which is shorter than its diff:
```python
import functools

import jax
import jax.numpy as jnp
from jax import lax
from jax.experimental import pallas as pl
from jax.experimental.pallas import tpu as pltpu
from jax.sharding import PartitionSpec as P

exchange_coef = -0.9847450218426965
lanes = 128
big_vmem = 60 * 1024 * 1024


def pack_kernel(groups, per, rows_ref, me_ref, coef_ref, *out_refs):
    me = me_ref[0]
    atoms, pad, _ = coef_ref.shape
    row = lax.broadcasted_iota(jnp.int32, (pad, lanes), 0)
    for d, out_ref in enumerate(out_refs):
        peer = me ^ d
        for q in range(per):
            k = peer * per + q
            start = pl.multiple_of(jnp.minimum(k, groups - 1) * lanes, lanes)
            for a in range(atoms):
                value = coef_ref[a, :, pl.ds(start, lanes)]
                limit = jnp.where(k < groups, rows_ref[a], 0)
                out_ref[a * pad : (a + 1) * pad, q * lanes : (q + 1) * lanes] = jnp.where(
                    row < limit, value, jnp.zeros_like(value)
                )


def unpack_kernel(groups, per, rows_ref, me_ref, *refs):
    in_refs, out_ref = refs[:-1], refs[-1]
    me = me_ref[0]
    atoms, pad, _ = out_ref.shape
    row = lax.broadcasted_iota(jnp.int32, (pad, lanes), 0)
    for d, in_ref in enumerate(in_refs):
        peer = me ^ d
        for q in range(per):
            k = peer * per + q

            @pl.when(k < groups)
            def _():
                start = pl.multiple_of(k * lanes, lanes)
                for a in range(atoms):
                    value = in_ref[a * pad : (a + 1) * pad, q * lanes : (q + 1) * lanes]
                    out_ref[a, :, pl.ds(start, lanes)] = jnp.where(
                        row < rows_ref[a], value.astype(jnp.float32), 0.0
                    )


def prep_kernel(piece, at_ref, touch_ref, rows_ref, outer_ref, basis_ref, out_ref, meta):
    beta = at_ref[1]
    tiles_dev, touch_len = touch_ref.shape
    atoms = rows_ref.shape[1]
    start = pl.multiple_of(beta * piece, piece)
    out_ref[:piece] = basis_ref[pl.ds(start, piece), :]
    meta[...] = jnp.zeros_like(meta)
    rest = outer_ref[...]
    for part in range(3):
        rounded = rest.astype(jnp.bfloat16).astype(jnp.float32)
        meta[part * tiles_dev : (part + 1) * tiles_dev, :] = rounded
        rest = rest - rounded
    ids = touch_ref[...]
    row = 3 * tiles_dev
    meta[row : row + tiles_dev, :touch_len] = (ids & 255).astype(jnp.float32)
    row += tiles_dev
    meta[row : row + tiles_dev, :touch_len] = (ids >> 8).astype(jnp.float32)
    row += tiles_dev
    meta[row : row + 1, :atoms] = rows_ref[...].astype(jnp.float32)
    out_ref[piece:] = meta[...].astype(jnp.bfloat16)


def load_all(block_refs, basis_refs, blocks, basis, sems):
    n, (low, m) = len(block_refs), basis.shape[:2]
    atoms = blocks.shape[0] // n
    copies = []
    for d, ref in enumerate(block_refs):
        copies.append(
            pltpu.make_async_copy(ref, blocks.at[pl.ds(d * atoms, atoms)], sems.at[d])
        )
    for y in range(low):
        for e in range(m):
            k = y * m + e
            copies.append(pltpu.make_async_copy(basis_refs[k], basis.at[y, e], sems.at[n + k]))
    for copy in copies:
        copy.start()
    for copy in copies:
        copy.wait()


def tile_blocks(touch_ref, me, index, blocks, atoms):
    touch_len = touch_ref.shape[1]
    return jnp.concatenate(
        [blocks[touch_ref[index, s] ^ (me * atoms)] for s in range(touch_len)], axis=0
    )


def tile_basis(beta, index, tiles_dev, piece, basis):
    low, m = basis.shape[:2]
    d, slot = index // tiles_dev, index % tiles_dev
    count = m // tiles_dev
    return jnp.concatenate(
        [basis[d % low, (slot * count + c) ^ beta, d // low, :piece] for c in range(count)], axis=0
    )


def global_tile(me, index, tiles_dev):
    return ((index // tiles_dev) ^ me) * tiles_dev + index % tiles_dev


def forward_kernel(n, k, tiles_dev, piece, scale, touch_ref, at_ref, weight_ref, *refs):
    block_refs, basis_refs = refs[:n], refs[n : n + k]
    out_ref, blocks, basis, sems = refs[n + k :]
    me, beta = at_ref[0], at_ref[1]
    tile_count = touch_ref.shape[0]
    atoms = blocks.shape[0] // n
    load_all(block_refs, basis_refs, blocks, basis, sems)

    def step(index, carry):
        part = tile_blocks(touch_ref, me, index, blocks, atoms)
        product = lax.dot_general(
            part,
            tile_basis(beta, index, tiles_dev, piece, basis),
            (((0,), (0,)), ((), ())),
            preferred_element_type=jnp.float32,
        )
        orbital = product.astype(jnp.bfloat16).astype(jnp.float32)
        out_ref[pl.ds(global_tile(me, index, tiles_dev), 1), :] = scale * jnp.sum(
            weight_ref[...] * orbital * orbital, axis=0, keepdims=True
        )
        return carry

    lax.fori_loop(0, tile_count, step, 0)


def backward_kernel(n, k, tiles_dev, piece, touch_ref, at_ref, weight_ref, outer_ref, local_ref, *refs):
    block_refs, basis_refs = refs[:n], refs[n : n + k]
    out_refs = refs[n + k : 2 * n + k]
    blocks, basis, total, sems = refs[2 * n + k :]
    me, beta = at_ref[0], at_ref[1]
    tile_count, touch_len = touch_ref.shape
    pad = blocks.shape[1]
    atoms = blocks.shape[0] // n
    load_all(block_refs, basis_refs, blocks, basis, sems)
    total[...] = jnp.zeros_like(total)

    def step(index, carry):
        part = tile_blocks(touch_ref, me, index, blocks, atoms)
        values = tile_basis(beta, index, tiles_dev, piece, basis)
        potential = (
            outer_ref[pl.ds(index, 1), :]
            + local_ref[pl.ds(global_tile(me, index, tiles_dev), 1), :]
        )
        scaled = (values.astype(jnp.float32) * potential).astype(jnp.bfloat16)
        couple = lax.dot_general(
            scaled, values, (((1,), (1,)), ((), ())), preferred_element_type=jnp.float32
        )
        high = couple.astype(jnp.bfloat16)
        low = (couple - high.astype(jnp.float32)).astype(jnp.bfloat16)
        product = jnp.dot(high, part, preferred_element_type=jnp.float32) + jnp.dot(
            low, part, preferred_element_type=jnp.float32
        )
        for s in range(touch_len):
            total[touch_ref[index, s] ^ (me * atoms)] += product[s * pad : (s + 1) * pad]
        return carry

    lax.fori_loop(0, tile_count, step, 0)
    weight = weight_ref[...]
    for d, out_ref in enumerate(out_refs):
        for a in range(atoms):
            out_ref[a * pad : (a + 1) * pad, :] = (total[d * atoms + a] * weight).astype(
                jnp.bfloat16
            )


smem = pl.BlockSpec(memory_space=pltpu.SMEM)
vmem = pl.BlockSpec(memory_space=pltpu.VMEM)
anywhere = pl.BlockSpec(memory_space=pl.ANY)


def swap(value, axis, offset):
    size = lax.axis_size(axis)
    return lax.ppermute(value, axis, [(i, i ^ offset) for i in range(size)])


def exchange(parts):
    return [parts[0]] + [swap(parts[d], "grid", d) for d in range(1, len(parts))]


def all_sum(value):
    for axis in ("band", "grid"):
        offset = 1
        while offset < lax.axis_size(axis):
            value = value + swap(value, axis, offset)
            offset *= 2
    return value


def body(coefficients, block_rows, touch_atoms, basis_values, outer_field, occupations):
    n = lax.axis_size("grid")
    m = lax.axis_size("band")
    me = lax.axis_index("grid").astype(jnp.int32)
    beta = lax.axis_index("band").astype(jnp.int32)
    atoms, pad, band_dev = coefficients.shape
    tiles_dev, touch_len = touch_atoms.shape
    points = basis_values.shape[2]
    slots = basis_values.shape[1]
    tile_count = tiles_dev * n
    groups = band_dev // lanes
    per = (groups + n - 1) // n
    width = per * lanes
    params = pltpu.CompilerParams(vmem_limit_bytes=big_vmem)
    at = jnp.stack([me, beta])

    piece = tiles_dev * slots // m
    extra = -(-(5 * tiles_dev + 1) // 16) * 16
    low = 1 << ((n.bit_length() - 1) // 2)
    message = pl.pallas_call(
        functools.partial(prep_kernel, piece),
        out_shape=jax.ShapeDtypeStruct((piece + extra, points), jnp.bfloat16),
        in_specs=[smem, vmem, vmem, vmem, vmem],
        out_specs=vmem,
        scratch_shapes=[pltpu.VMEM((extra, points), jnp.float32)],
        compiler_params=params,
        name="prep",
    )(
        at,
        touch_atoms,
        block_rows.reshape(1, atoms),
        outer_field,
        basis_values.reshape(tiles_dev * slots, points),
    )
    column = [message] + [swap(message, "grid", low * k) for k in range(1, n // low)]

    sent = pl.pallas_call(
        functools.partial(pack_kernel, groups, per),
        out_shape=[jax.ShapeDtypeStruct((atoms * pad, width), jnp.bfloat16)] * n,
        in_specs=[smem, smem, vmem],
        out_specs=[vmem] * n,
        compiler_params=params,
        name="pack",
    )(block_rows, at, coefficients)
    column, sent = lax.optimization_barrier((jnp.stack(column), sent))
    pieces = {(0, 0): column}
    for x in range(2, m, 2):
        pieces[0, x] = swap(column, "band", x)
    for y in range(1, low):
        pieces[y, 0] = swap(column, "grid", y)
    got = [item.reshape(atoms, pad, width) for item in exchange(sent)]
    for y in range(1, low):
        for x in range(2, m, 2):
            pieces[y, x] = swap(pieces[0, x], "grid", y)
    for y, x in list(pieces):
        pieces[y, x + 1] = swap(pieces[y, x], "band", 1)
    basis = [pieces[y, e] for y in range(low) for e in range(m)]
    tables = jnp.stack([pieces[d % low, 0][d // low, piece:] for d in range(n)]).astype(jnp.float32)
    part = tables[:, : 3 * tiles_dev].reshape(n, 3, tiles_dev, points)
    outer = (part[:, 0] + part[:, 1] + part[:, 2]).reshape(tile_count, points)
    ids = tables[:, 3 * tiles_dev : 5 * tiles_dev, :touch_len].reshape(n, 2, tiles_dev, touch_len)
    touch = (ids[:, 0] + 256.0 * ids[:, 1]).astype(jnp.int32).reshape(tile_count, touch_len)

    filled = jnp.pad(occupations, (0, n * width - band_dev))
    weight = lax.dynamic_slice_in_dim(filled, me * width, width, 0)
    all_bands = band_dev * m
    scratch = [
        pltpu.VMEM((n * atoms, pad, width), jnp.bfloat16),
        pltpu.VMEM((low, m, n // low, piece + extra, points), jnp.bfloat16),
    ]
    count = low * m
    sems = pltpu.SemaphoreType.DMA((n + count,))
    partial_value = pl.pallas_call(
        functools.partial(forward_kernel, n, count, tiles_dev, piece, 1.0 / all_bands),
        out_shape=jax.ShapeDtypeStruct((tile_count, points), jnp.float32),
        in_specs=[smem, smem, vmem] + [anywhere] * (n + count),
        out_specs=vmem,
        scratch_shapes=scratch + [sems],
        compiler_params=params,
        name="forward",
    )(touch, at, weight[:, None], *got, *basis)
    density = all_sum(partial_value)
    local = exchange_coef * jnp.cbrt(density)
    back = pl.pallas_call(
        functools.partial(backward_kernel, n, count, tiles_dev, piece),
        out_shape=[jax.ShapeDtypeStruct((atoms * pad, width), jnp.bfloat16)] * n,
        in_specs=[smem, smem, vmem, vmem, vmem] + [anywhere] * (n + count),
        out_specs=[vmem] * n,
        scratch_shapes=scratch + [pltpu.VMEM((n * atoms, pad, width), jnp.float32), sems],
        compiler_params=params,
        name="backward",
    )(touch, at, weight[None, :], outer, local, *got, *basis)
    returned = exchange(back)
    gradient = pl.pallas_call(
        functools.partial(unpack_kernel, groups, per),
        out_shape=jax.ShapeDtypeStruct((atoms, pad, band_dev), jnp.float32),
        in_specs=[smem, smem] + [vmem] * n,
        out_specs=vmem,
        compiler_params=params,
        name="unpack",
    )(block_rows, at, *returned)
    own_density = lax.dynamic_slice_in_dim(density, me * tiles_dev, tiles_dev, 0)
    return (gradient, own_density)


def solution(mesh):
    placed = (
        P("grid", None, "band"),
        P("grid"),
        P("grid", None),
        P("grid", None, None),
        P("grid", None),
        P("band"),
    )
    return jax.shard_map(
        body,
        mesh=mesh,
        in_specs=placed,
        out_specs=(P("grid", None, "band"), P("grid", None)),
        check_vma=False,
    )
```

time: 262 us -> 193 us (0.74)
  blocking collectives: 94.7 us -> 0 us
  starting transfers between devices: 23.1 us -> 33.5 us
  waiting for transfers between devices: 99.3 us -> 109 us
    all_gather x2 -> x0, blocking collectives: 58.2 us -> none  [the longest x1 29.3 us: body(): touch_all = lax.all_gather(touch_atoms, 'grid', axis=0, tiled=True)]
    all_to_all x1 -> x0, blocking collectives: 36.5 us -> none  [body(): lax.all_to_all(jnp.broadcast_to(own[None], (n, piece, points)), 'grid', s...]
    ppermute x22 -> x29, starting transfers between devices: 23.1 us -> 33.5 us  [swap(): return lax.ppermute(value, axis, [(i, i ^ offset) for i in range(size)])]
    ppermute x22 -> x29, waiting for transfers between devices: 99.3 us -> 109 us  [swap(): return lax.ppermute(value, axis, [(i, i ^ offset) for i in range(size)])]
    pallas_call x2 -> x3, Pallas kernels: 29.4 us -> 31.9 us  [the longest x1 17.9 us: body(): pl.pallas_call(functools.partial(backward_kernel, n, count, tiles_dev, pi...]
  transfers between devices with their start and end apart: 22 -> 29, of which waited for: 15 -> 21; matrix products, arithmetic and copies ran while one was open for 1% -> 2% of each run, Pallas kernels for 1% -> 2%
where the time goes in v2:
time: 193 us; the launch traced here: 192 us
  waiting for transfers between devices  109 us (56%)
  Pallas kernels  39.2 us (20%)
  starting transfers between devices  33.5 us (17%)
  local copies, waits for them, and re-layouts  5.83 us (3%)
  other arithmetic  3.75 us (2%)
    ppermute x29, waiting for transfers between devices, swap(): return lax.ppermute(value, axis, [(i, i ^ offset) for i in range(size)])  109 us
    ppermute x29, starting transfers between devices, swap(): return lax.ppermute(value, axis, [(i, i ^ offset) for i in range(size)])  33.5 us
    pallas_call x1, Pallas kernels, body(): pl.pallas_call(functools.partial(backward_kernel, n, count, tiles_dev, pi...  17.9 us
    pallas_call x1, Pallas kernels, body(): pl.pallas_call(functools.partial(forward_kernel, n, count, tiles_dev, pie...  12.1 us
    pallas_call x1, Pallas kernels, body(): pl.pallas_call(functools.partial(unpack_kernel, groups, per), out_shape=j...  4.04 us
  transfers between devices with their start and end apart: 29, of which 21 were waited for; matrix products, arithmetic and copies ran while one was open for 2% of the time, Pallas kernels for 2%

profile of v2, /device:TPU:8, one launch (start us, length us, event | category | flops | bytes accessed | tf_op | source)
XLA Modules:
  0.0 192.4 jit_solution(3445984612523310032)
XLA Ops:
  7.1 3.3 %pack.1 = (bf16[256,512]{1,0:T(8,128)(2,1)}, bf16[256,512]{1,0:T(8,128)(2,1)}, bf16[256,512]{1,0:T(8,128)(2,1)}, bf16[256,512]{1,0:T(8,128)(2,1)}, bf16[256,512]...) custom-call(s32[16]{0:T(128)} %rows_ref.3, ...), custom_call_target="tpu_custom_call" | custom-call | tf_op jit(solution)/shard_map/pack/pallas_call | solution.py:236
  10.5 8.1 %collective-permute-done.2 = bf16[144,640]{1,0:T(8,128)(2,1)S(1)} collective-permute-done((bf16[144,640]{1,0:T(8,128)(2,1)}, bf16[144,640]{1,0:T(8,128)(2,1)S(1)}, u32[]{:S(2)}, u32[]{:S(2)}) %collective-permute-start.2) | collective-permute-done | bytes 184352 | tf_op jit(solution)/shard_map/ppermute | solution.py:184
  29.6 9.7 %collective-permute-done.12.refs_10_ = bf16[4,144,640]{2,1,0:T(8,128)(2,1)S(1)} collective-permute-done((bf16[4,144,640]{2,1,0:T(8,128)(2,1)S(1)}, bf16[4,144,640]{2,1,0:T(8,128)(2,1)S(1)}, u32[]{:S(2)}, u32[]{:S(2)}) %collective-permute-start.12) | collective-permute-done | bytes 737312 | tf_op jit(solution)/shard_map/ppermute | solution.py:184
  39.2 3.3 %collective-permute-start.7 = (bf16[256,512]{1,0:T(8,128)(2,1)}, bf16[256,512]{1,0:T(8,128)(2,1)S(1)}, u32[]{:S(2)}, u32[]{:S(2)}) collective-permute-start(bf16[256,512]{1,0:T(8,128)(2,1)} %get-tuple-element.40), channel_id=1, source_target_pairs={{0,4},{1,5},{2,6},{3,7},{4,0},{5,1},{6,2},{7,3},{8,12},{9,13},{10,... | collective-permute-start | bytes 786440 | tf_op jit(solution)/shard_map/ppermute | solution.py:184
  42.5 5.9 %collective-permute-done.3.refs_12_ = bf16[4,144,640]{2,1,0:T(8,128)(2,1)S(1)} collective-permute-done((bf16[4,144,640]{2,1,0:T(8,128)(2,1)S(1)}, bf16[4,144,640]{2,1,0:T(8,128)(2,1)S(1)}, u32[]{:S(2)}, u32[]{:S(2)}) %collective-permute-start.3) | collective-permute-done | bytes 737312 | tf_op jit(solution)/shard_map/ppermute | solution.py:184
  49.9 4.1 %collective-permute-done.4 = bf16[256,512]{1,0:T(8,128)(2,1)S(1)} collective-permute-done((bf16[256,512]{1,0:T(8,128)(2,1)}, bf16[256,512]{1,0:T(8,128)(2,1)S(1)}, u32[]{:S(2)}, u32[]{:S(2)}) %collective-permute-start.4) | collective-permute-done | bytes 262176 | tf_op jit(solution)/shard_map/ppermute | solution.py:184
  54.0 4.2 %collective-permute-start.8 = (bf16[256,512]{1,0:T(8,128)(2,1)}, bf16[256,512]{1,0:T(8,128)(2,1)S(1)}, u32[]{:S(2)}, u32[]{:S(2)}) collective-permute-start(bf16[256,512]{1,0:T(8,128)(2,1)} %get-tuple-element.41), channel_id=1, source_target_pairs={{0,5},{1,4},{2,7},{3,6},{4,1},{5,0},{6,3},{7,2},{8,13},{9,12},{10,... | collective-permute-start | bytes 786440 | tf_op jit(solution)/shard_map/ppermute | solution.py:184
  59.0 12.9 %collective-permute-done.8 = bf16[256,512]{1,0:T(8,128)(2,1)S(1)} collective-permute-done((bf16[256,512]{1,0:T(8,128)(2,1)}, bf16[256,512]{1,0:T(8,128)(2,1)S(1)}, u32[]{:S(2)}, u32[]{:S(2)}) %collective-permute-start.8) | collective-permute-done | bytes 262176 | tf_op jit(solution)/shard_map/ppermute | solution.py:184
  73.1 3.5 %collective-permute-done.9 = bf16[256,512]{1,0:T(8,128)(2,1)S(1)} collective-permute-done((bf16[256,512]{1,0:T(8,128)(2,1)}, bf16[256,512]{1,0:T(8,128)(2,1)S(1)}, u32[]{:S(2)}, u32[]{:S(2)}) %collective-permute-start.9) | collective-permute-done | bytes 262176 | tf_op jit(solution)/shard_map/ppermute | solution.py:184
  78.7 10.1 %collective-permute-done.10 = bf16[256,512]{1,0:T(8,128)(2,1)S(1)} collective-permute-done((bf16[256,512]{1,0:T(8,128)(2,1)}, bf16[256,512]{1,0:T(8,128)(2,1)S(1)}, u32[]{:S(2)}, u32[]{:S(2)}) %collective-permute-start.10) | collective-permute-done | bytes 262176 | tf_op jit(solution)/shard_map/ppermute | solution.py:184
  90.8 12.1 %forward.1 = f32[16,640]{1,0:T(8,128)} custom-call(s32[16,16]{1,0:T(8,128)} %bitcast.45, s32[2]{0:T(128)} %pad_add_fusion.at_ref.me_ref, f32[512,1]{1,0:T(8,128)} %copy.10.weight_ref, bf16[16,16,512]{2,1,0:T(8,128)(2,1)} %bitcast.23, bf16[16,16,512]{2,1,0:T(8,128)(2,1)} %bitcast.25, bf16[16,16,512]{2,1,0:T(8,128)(2,1)} %bitcast.27, ...), custom_call_target="tpu_custom_call" | custom-call | tf_op jit(solution)/shard_map/forward/pallas_call | solution.py:272
  105.7 3.5 %collective-permute-done.18 = f32[16,640]{1,0:T(8,128)S(1)} collective-permute-done((f32[16,640]{1,0:T(8,128)S(1)}, f32[16,640]{1,0:T(8,128)S(1)}, u32[]{:S(2)}, u32[]{:S(2)}) %collective-permute-start.18) | collective-permute-done | bytes 40992 | tf_op jit(solution)/shard_map/ppermute | solution.py:184
  110.6 2.6 %collective-permute-done.19 = f32[16,640]{1,0:T(8,128)S(1)} collective-permute-done((f32[16,640]{1,0:T(8,128)S(1)}, f32[16,640]{1,0:T(8,128)S(1)}, u32[]{:S(2)}, u32[]{:S(2)}) %collective-permute-start.19) | collective-permute-done | bytes 40992 | tf_op jit(solution)/shard_map/ppermute | solution.py:184
  114.2 3.2 %collective-permute-done.20 = f32[16,640]{1,0:T(8,128)S(1)} collective-permute-done((f32[16,640]{1,0:T(8,128)S(1)}, f32[16,640]{1,0:T(8,128)S(1)}, u32[]{:S(2)}, u32[]{:S(2)}) %collective-permute-start.20) | collective-permute-done | bytes 40992 | tf_op jit(solution)/shard_map/ppermute | solution.py:184
  118.5 3.8 %collective-permute-done.21 = f32[16,640]{1,0:T(8,128)S(1)} collective-permute-done((f32[16,640]{1,0:T(8,128)S(1)}, f32[16,640]{1,0:T(8,128)S(1)}, u32[]{:S(2)}, u32[]{:S(2)}) %collective-permute-start.21) | collective-permute-done | bytes 40992 | tf_op jit(solution)/shard_map/ppermute | solution.py:184
  123.0 17.9 %backward.1 = (bf16[256,512]{1,0:T(8,128)(2,1)}, bf16[256,512]{1,0:T(8,128)(2,1)}, bf16[256,512]{1,0:T(8,128)(2,1)}, bf16[256,512]{1,0:T(8,128)(2,1)}, bf16[256,...) custom-call(s32[16,16]{1,0:T(8,128)} %bitcast.46, ...), custom_call_target="tpu_custom_call" | custom-call | tf_op jit(solution)/shard_map/backward/pallas_call | solution.py:283
  145.3 2.7 %collective-permute-start.26 = (bf16[256,512]{1,0:T(8,128)(2,1)}, bf16[256,512]{1,0:T(8,128)(2,1)S(1)}, u32[]{:S(2)}, u32[]{:S(2)}) collective-permute-start(bf16[256,512]{1,0:T(8,128)(2,1)} %get-tuple-element.49), channel_id=1, source_target_pairs={{0,5},{1,4},{2,7},{3,6},{4,1},{5,0},{6,3},{7,2},{8,13},{9,12},{10,... | collective-permute-start | bytes 786440 | tf_op jit(solution)/shard_map/ppermute | solution.py:184
  150.0 4.0 %collective-permute-done.23.refs_2_ = bf16[256,512]{1,0:T(8,128)(2,1)S(1)} collective-permute-done((bf16[256,512]{1,0:T(8,128)(2,1)}, bf16[256,512]{1,0:T(8,128)(2,1)S(1)}, u32[]{:S(2)}, u32[]{:S(2)}) %collective-permute-start.23) | collective-permute-done | bytes 262176 | tf_op jit(solution)/shard_map/ppermute | solution.py:184
  155.6 3.6 %collective-permute-done.24.refs_3_ = bf16[256,512]{1,0:T(8,128)(2,1)S(1)} collective-permute-done((bf16[256,512]{1,0:T(8,128)(2,1)}, bf16[256,512]{1,0:T(8,128)(2,1)S(1)}, u32[]{:S(2)}, u32[]{:S(2)}) %collective-permute-start.24) | collective-permute-done | bytes 262176 | tf_op jit(solution)/shard_map/ppermute | solution.py:184
  159.3 15.0 %collective-permute-done.25.refs_4_ = bf16[256,512]{1,0:T(8,128)(2,1)S(1)} collective-permute-done((bf16[256,512]{1,0:T(8,128)(2,1)}, bf16[256,512]{1,0:T(8,128)(2,1)S(1)}, u32[]{:S(2)}, u32[]{:S(2)}) %collective-permute-start.25) | collective-permute-done | bytes 262176 | tf_op jit(solution)/shard_map/ppermute | solution.py:184
  174.2 5.6 %collective-permute-done.26.refs_5_ = bf16[256,512]{1,0:T(8,128)(2,1)S(1)} collective-permute-done((bf16[256,512]{1,0:T(8,128)(2,1)}, bf16[256,512]{1,0:T(8,128)(2,1)S(1)}, u32[]{:S(2)}, u32[]{:S(2)}) %collective-permute-start.26) | collective-permute-done | bytes 262176 | tf_op jit(solution)/shard_map/ppermute | solution.py:184
  179.8 4.3 %collective-permute-done.27.refs_6_ = bf16[256,512]{1,0:T(8,128)(2,1)S(1)} collective-permute-done((bf16[256,512]{1,0:T(8,128)(2,1)}, bf16[256,512]{1,0:T(8,128)(2,1)S(1)}, u32[]{:S(2)}, u32[]{:S(2)}) %collective-permute-start.27) | collective-permute-done | bytes 262176 | tf_op jit(solution)/shard_map/ppermute | solution.py:184
  184.1 3.5 %collective-permute-done.28.refs_7_ = bf16[256,512]{1,0:T(8,128)(2,1)S(1)} collective-permute-done((bf16[256,512]{1,0:T(8,128)(2,1)}, bf16[256,512]{1,0:T(8,128)(2,1)S(1)}, u32[]{:S(2)}, u32[]{:S(2)}) %collective-permute-start.28) | collective-permute-done | bytes 262176 | tf_op jit(solution)/shard_map/ppermute | solution.py:184
  188.3 4.0 %unpack.1 = f32[16,16,3840]{2,1,0:T(8,128)} custom-call(s32[16]{0:T(128)} %rows_ref.3, s32[2]{0:T(128)} %pad_add_fusion.at_ref.me_ref, bf16[256,512]{1,0:T(8,128)(2,1)} %get-tuple-element.44.refs_0_, bf16[256,512]{1,0:T(8,128)(2,1)} %copy-done.15, bf16[256,512]{1,0:T(8,128)(2,1)} %copy-done.16, bf16[256,512]{1,0:T(8,128)(2,1)} %copy-done.17, ...), custom_call_target="tpu_custom_call" | custom-call | tf_op jit(solution)/shard_map/unpack/pallas_call | solution.py:293
  (114 shorter events, 40.6 us)
Async XLA Ops:
  3.1 15.4 %collective-permute-start.2 = (bf16[144,640]{1,0:T(8,128)(2,1)}, bf16[144,640]{1,0:T(8,128)(2,1)S(1)}, u32[]{:S(2)}, u32[]{:S(2)}) collective-permute-start(bf16[144,640]{1,0:T(8,128)(2,1)} %prep.1), channel_id=1, source_target_pairs={{0,6},{1,7},{2,4},{3,5},{4,2},{5,3},{6,0},{7,1},{8,14},{9,15},{10,... | collective-permute-start | bytes 552968 | tf_op jit(solution)/shard_map/ppermute | solution.py:184
  4.7 16.1 %collective-permute-start.1 = (bf16[144,640]{1,0:T(8,128)(2,1)}, bf16[144,640]{1,0:T(8,128)(2,1)S(1)}, u32[]{:S(2)}, u32[]{:S(2)}) collective-permute-start(bf16[144,640]{1,0:T(8,128)(2,1)} %prep.1), channel_id=1, source_target_pairs={{0,4},{1,5},{2,6},{3,7},{4,0},{5,1},{6,2},{7,3},{8,12},{9,13},{10,... | collective-permute-start | bytes 552968 | tf_op jit(solution)/shard_map/ppermute | solution.py:184
  5.7 15.0 %collective-permute-start = (bf16[144,640]{1,0:T(8,128)(2,1)}, bf16[144,640]{1,0:T(8,128)(2,1)S(1)}, u32[]{:S(2)}, u32[]{:S(2)}) collective-permute-start(bf16[144,640]{1,0:T(8,128)(2,1)} %prep.1), channel_id=1, source_target_pairs={{0,2},{1,3},{2,0},{3,1},{4,6},{5,7},{6,4},{7,5},{8,10},{9,11},{10,... | collective-permute-start | bytes 552968 | tf_op jit(solution)/shard_map/ppermute | solution.py:184
  21.8 17.4 %collective-permute-start.12 = (bf16[4,144,640]{2,1,0:T(8,128)(2,1)S(1)}, bf16[4,144,640]{2,1,0:T(8,128)(2,1)S(1)}, u32[]{:S(2)}, u32[]{:S(2)}) collective-permute-start(bf16[4,144,640]{2,1,0:T(8,128)(2,1)S(1)} %pad_maximum_fusion.refs_8_), channel_id=1, source_target_pairs={{0,16},{8,24},{16,0},{24,8},{1,17},{9,25},{17,1},{25,9},{2,18},{10... | collective-permute-start | bytes 2211848 | tf_op jit(solution)/shard_map/ppermute | solution.py:184
  23.3 25.0 %collective-permute-start.3 = (bf16[4,144,640]{2,1,0:T(8,128)(2,1)S(1)}, bf16[4,144,640]{2,1,0:T(8,128)(2,1)S(1)}, u32[]{:S(2)}, u32[]{:S(2)}) collective-permute-start(bf16[4,144,640]{2,1,0:T(8,128)(2,1)S(1)} %pad_maximum_fusion.refs_8_), channel_id=1, source_target_pairs={{0,1},{1,0},{2,3},{3,2},{4,5},{5,4},{6,7},{7,6},{8,9},{9,8},{10,11... | collective-permute-start | bytes 2211848 | tf_op jit(solution)/shard_map/ppermute | solution.py:184
  25.8 28.2 %collective-permute-start.4 = (bf16[256,512]{1,0:T(8,128)(2,1)}, bf16[256,512]{1,0:T(8,128)(2,1)S(1)}, u32[]{:S(2)}, u32[]{:S(2)}) collective-permute-start(bf16[256,512]{1,0:T(8,128)(2,1)} %get-tuple-element.37), channel_id=1, source_target_pairs={{0,1},{1,0},{2,3},{3,2},{4,5},{5,4},{6,7},{7,6},{8,9},{9,8},{10,11... | collective-permute-start | bytes 786440 | tf_op jit(solution)/shard_map/ppermute | solution.py:184
  26.3 31.9 %collective-permute-start.5 = (bf16[256,512]{1,0:T(8,128)(2,1)}, bf16[256,512]{1,0:T(8,128)(2,1)S(1)}, u32[]{:S(2)}, u32[]{:S(2)}) collective-permute-start(bf16[256,512]{1,0:T(8,128)(2,1)} %get-tuple-element.38), channel_id=1, source_target_pairs={{0,2},{1,3},{2,0},{3,1},{4,6},{5,7},{6,4},{7,5},{8,10},{9,11},{10,... | collective-permute-start | bytes 786440 | tf_op jit(solution)/shard_map/ppermute | solution.py:184
  28.6 29.8 %collective-permute-start.6 = (bf16[256,512]{1,0:T(8,128)(2,1)}, bf16[256,512]{1,0:T(8,128)(2,1)S(1)}, u32[]{:S(2)}, u32[]{:S(2)}) collective-permute-start(bf16[256,512]{1,0:T(8,128)(2,1)} %get-tuple-element.39), channel_id=1, source_target_pairs={{0,3},{1,2},{2,1},{3,0},{4,7},{5,6},{6,5},{7,4},{8,11},{9,10},{10,... | collective-permute-start | bytes 786440 | tf_op jit(solution)/shard_map/ppermute | solution.py:184
  39.2 19.7 %collective-permute-start.7 = (bf16[256,512]{1,0:T(8,128)(2,1)}, bf16[256,512]{1,0:T(8,128)(2,1)S(1)}, u32[]{:S(2)}, u32[]{:S(2)}) collective-permute-start(bf16[256,512]{1,0:T(8,128)(2,1)} %get-tuple-element.40), channel_id=1, source_target_pairs={{0,4},{1,5},{2,6},{3,7},{4,0},{5,1},{6,2},{7,3},{8,12},{9,13},{10,... | collective-permute-start | bytes 786440 | tf_op jit(solution)/shard_map/ppermute | solution.py:184
  48.4 24.7 %collective-permute-start.15 = (bf16[4,144,640]{2,1,0:T(8,128)(2,1)S(1)}, bf16[4,144,640]{2,1,0:T(8,128)(2,1)S(1)}, u32[]{:S(2)}, u32[]{:S(2)}) collective-permute-start(bf16[4,144,640]{2,1,0:T(8,128)(2,1)S(1)} %collective-permute-done.12.refs_10_), channel_id=1, source_target_pairs={{0,1},{1,0},{2,3},{3,2},{4,5},{5,4},{6,7},{7,6},{8,9},{9,8},{10,11... | collective-permute-start | bytes 2211848 | tf_op jit(solution)/shard_map/ppermute | solution.py:184
  54.0 17.9 %collective-permute-start.8 = (bf16[256,512]{1,0:T(8,128)(2,1)}, bf16[256,512]{1,0:T(8,128)(2,1)S(1)}, u32[]{:S(2)}, u32[]{:S(2)}) collective-permute-start(bf16[256,512]{1,0:T(8,128)(2,1)} %get-tuple-element.41), channel_id=1, source_target_pairs={{0,5},{1,4},{2,7},{3,6},{4,1},{5,0},{6,3},{7,2},{8,13},{9,12},{10,... | collective-permute-start | bytes 786440 | tf_op jit(solution)/shard_map/ppermute | solution.py:184
  58.3 30.6 %collective-permute-start.11 = (bf16[4,144,640]{2,1,0:T(8,128)(2,1)S(1)}, bf16[4,144,640]{2,1,0:T(8,128)(2,1)S(1)}, u32[]{:S(2)}, u32[]{:S(2)}) collective-permute-start(bf16[4,144,640]{2,1,0:T(8,128)(2,1)S(1)} %pad_maximum_fusion.refs_8_), channel_id=1, source_target_pairs={{0,8},{8,0},{16,24},{24,16},{1,9},{9,1},{17,25},{25,17},{2,10},{10... | collective-permute-start | bytes 2211848 | tf_op jit(solution)/shard_map/ppermute | solution.py:184
  58.4 18.2 %collective-permute-start.9 = (bf16[256,512]{1,0:T(8,128)(2,1)}, bf16[256,512]{1,0:T(8,128)(2,1)S(1)}, u32[]{:S(2)}, u32[]{:S(2)}) collective-permute-start(bf16[256,512]{1,0:T(8,128)(2,1)} %get-tuple-element.42), channel_id=1, source_target_pairs={{0,6},{1,7},{2,4},{3,5},{4,2},{5,3},{6,0},{7,1},{8,14},{9,15},{10,... | collective-permute-start | bytes 786440 | tf_op jit(solution)/shard_map/ppermute | solution.py:184
  58.9 29.9 %collective-permute-start.13 = (bf16[4,144,640]{2,1,0:T(8,128)(2,1)S(1)}, bf16[4,144,640]{2,1,0:T(8,128)(2,1)S(1)}, u32[]{:S(2)}, u32[]{:S(2)}) collective-permute-start(bf16[4,144,640]{2,1,0:T(8,128)(2,1)S(1)} %collective-permute-done.12.refs_10_), channel_id=1, source_target_pairs={{0,8},{8,0},{16,24},{24,16},{1,9},{9,1},{17,25},{25,17},{2,10},{10... | collective-permute-start | bytes 2211848 | tf_op jit(solution)/shard_map/ppermute | solution.py:184
  71.9 16.9 %collective-permute-start.14 = (bf16[4,144,640]{2,1,0:T(8,128)(2,1)S(1)}, bf16[4,144,640]{2,1,0:T(8,128)(2,1)S(1)}, u32[]{:S(2)}, u32[]{:S(2)}) collective-permute-start(bf16[4,144,640]{2,1,0:T(8,128)(2,1)S(1)} %collective-permute-done.3.refs_12_), channel_id=1, source_target_pairs={{0,8},{8,0},{16,24},{24,16},{1,9},{9,1},{17,25},{25,17},{2,10},{10... | collective-permute-start | bytes 2211848 | tf_op jit(solution)/shard_map/ppermute | solution.py:184
  73.1 15.8 %collective-permute-start.16 = (bf16[4,144,640]{2,1,0:T(8,128)(2,1)S(1)}, bf16[4,144,640]{2,1,0:T(8,128)(2,1)S(1)}, u32[]{:S(2)}, u32[]{:S(2)}) collective-permute-start(bf16[4,144,640]{2,1,0:T(8,128)(2,1)S(1)} %collective-permute-done.15.refs_14_), channel_id=1, source_target_pairs={{0,8},{8,0},{16,24},{24,16},{1,9},{9,1},{17,25},{25,17},{2,10},{10... | collective-permute-start | bytes 2211848 | tf_op jit(solution)/shard_map/ppermute | solution.py:184
  76.6 12.2 %collective-permute-start.10 = (bf16[256,512]{1,0:T(8,128)(2,1)}, bf16[256,512]{1,0:T(8,128)(2,1)S(1)}, u32[]{:S(2)}, u32[]{:S(2)}) collective-permute-start(bf16[256,512]{1,0:T(8,128)(2,1)} %get-tuple-element.43), channel_id=1, source_target_pairs={{0,7},{1,6},{2,5},{3,4},{4,3},{5,2},{6,1},{7,0},{8,15},{9,14},{10,... | collective-permute-start | bytes 786440 | tf_op jit(solution)/shard_map/ppermute | solution.py:184
  140.9 8.3 %collective-permute-start.22 = (bf16[256,512]{1,0:T(8,128)(2,1)}, bf16[256,512]{1,0:T(8,128)(2,1)S(1)}, u32[]{:S(2)}, u32[]{:S(2)}) collective-permute-start(bf16[256,512]{1,0:T(8,128)(2,1)} %get-tuple-element.45), channel_id=1, source_target_pairs={{0,1},{1,0},{2,3},{3,2},{4,5},{5,4},{6,7},{7,6},{8,9},{9,8},{10,11... | collective-permute-start | bytes 786440 | tf_op jit(solution)/shard_map/ppermute | solution.py:184
  142.1 11.8 %collective-permute-start.23 = (bf16[256,512]{1,0:T(8,128)(2,1)}, bf16[256,512]{1,0:T(8,128)(2,1)S(1)}, u32[]{:S(2)}, u32[]{:S(2)}) collective-permute-start(bf16[256,512]{1,0:T(8,128)(2,1)} %get-tuple-element.46), channel_id=1, source_target_pairs={{0,2},{1,3},{2,0},{3,1},{4,6},{5,7},{6,4},{7,5},{8,10},{9,11},{10,... | collective-permute-start | bytes 786440 | tf_op jit(solution)/shard_map/ppermute | solution.py:184
  142.3 16.9 %collective-permute-start.24 = (bf16[256,512]{1,0:T(8,128)(2,1)}, bf16[256,512]{1,0:T(8,128)(2,1)S(1)}, u32[]{:S(2)}, u32[]{:S(2)}) collective-permute-start(bf16[256,512]{1,0:T(8,128)(2,1)} %get-tuple-element.47), channel_id=1, source_target_pairs={{0,3},{1,2},{2,1},{3,0},{4,7},{5,6},{6,5},{7,4},{8,11},{9,10},{10,... | collective-permute-start | bytes 786440 | tf_op jit(solution)/shard_map/ppermute | solution.py:184
  144.4 29.8 %collective-permute-start.25 = (bf16[256,512]{1,0:T(8,128)(2,1)}, bf16[256,512]{1,0:T(8,128)(2,1)S(1)}, u32[]{:S(2)}, u32[]{:S(2)}) collective-permute-start(bf16[256,512]{1,0:T(8,128)(2,1)} %get-tuple-element.48), channel_id=1, source_target_pairs={{0,4},{1,5},{2,6},{3,7},{4,0},{5,1},{6,2},{7,3},{8,12},{9,13},{10,... | collective-permute-start | bytes 786440 | tf_op jit(solution)/shard_map/ppermute | solution.py:184
  145.3 34.5 %collective-permute-start.26 = (bf16[256,512]{1,0:T(8,128)(2,1)}, bf16[256,512]{1,0:T(8,128)(2,1)S(1)}, u32[]{:S(2)}, u32[]{:S(2)}) collective-permute-start(bf16[256,512]{1,0:T(8,128)(2,1)} %get-tuple-element.49), channel_id=1, source_target_pairs={{0,5},{1,4},{2,7},{3,6},{4,1},{5,0},{6,3},{7,2},{8,13},{9,12},{10,... | collective-permute-start | bytes 786440 | tf_op jit(solution)/shard_map/ppermute | solution.py:184
  149.2 34.9 %collective-permute-start.27 = (bf16[256,512]{1,0:T(8,128)(2,1)}, bf16[256,512]{1,0:T(8,128)(2,1)S(1)}, u32[]{:S(2)}, u32[]{:S(2)}) collective-permute-start(bf16[256,512]{1,0:T(8,128)(2,1)} %get-tuple-element.50), channel_id=1, source_target_pairs={{0,6},{1,7},{2,4},{3,5},{4,2},{5,3},{6,0},{7,1},{8,14},{9,15},{10,... | collective-permute-start | bytes 786440 | tf_op jit(solution)/shard_map/ppermute | solution.py:184
  154.0 33.6 %collective-permute-start.28 = (bf16[256,512]{1,0:T(8,128)(2,1)}, bf16[256,512]{1,0:T(8,128)(2,1)S(1)}, u32[]{:S(2)}, u32[]{:S(2)}) collective-permute-start(bf16[256,512]{1,0:T(8,128)(2,1)} %get-tuple-element.51), channel_id=1, source_target_pairs={{0,7},{1,6},{2,5},{3,4},{4,3},{5,2},{6,1},{7,0},{8,15},{9,14},{10,... | collective-permute-start | bytes 786440 | tf_op jit(solution)/shard_map/ppermute | solution.py:184
  (30 other events, 613.3 us)
